TPU v7x, 32 devices: a whole 2x2x4 slice. The times are simulated.
32 devices in a mesh: ctx: 8 (over z, x), head: 4 (over y, core).
Axes of the slice: x: 2, y: 2, z: 4, core: 2. Of those that a mesh axis runs over, the one named last changes fastest.
Arguments:
- queries: bfloat16 [1024, 8192], P('ctx', 'head'), may hold values from -110 to 110
- key_heads: bfloat16 [1024, 1024], P('ctx'), may hold values from -4.61 to 4.61
- value_heads: bfloat16 [1024, 1024], P('ctx'), may hold values from -6 to 6
- span_order: int32 [16], replicated, may hold values from 0 to 15, each once
- block_mask: int32 [16, 16], replicated, may hold values 0 or 1
- mamba_in: bfloat16 [1024, 16384], P('ctx', 'head'), may hold values from -6 to 6
- gate_in: bfloat16 [1024, 16384], P('ctx', 'head'), may hold values from -6 to 6
- conv_weight: float32 [4, 16384], P(None, 'head'), may hold values from -3 to 3
- conv_bias: float32 [16384], P('head'), may hold values from -3 to 3
- low_weight: bfloat16 [16384, 512], P('head'), may hold values from -0.046875 to 0.046875
- bc_weight: bfloat16 [16384, 32], P('head'), may hold values from -0.046875 to 0.046875
- low_gain: float32 [512], replicated, may hold values from 0.1 to 1.9
- dt_weight: bfloat16 [512, 16384], P(None, 'head'), may hold values from -0.25 to 0.25
- dt_bias: float32 [16384], P('head'), may hold values from -7 to -2
- rate_log: float32 [16384, 16], P('head'), may hold values from -3 to 2.77
- skip_gain: float32 [16384], P('head'), may hold values from 0.5 to 1.5
Outputs:
- attn_out: bfloat16 [1024, 8192], P('ctx', 'head')
- mamba_out: bfloat16 [1024, 16384], P('ctx', 'head')
Inputs may be any that keep to these rules, and one draw needn't show every extreme that they name: `span_order`: each of the 16 span numbers stands in exactly one slot.
All inputs are finite; a program needn't handle non-finite values.
Results may differ from a plain program's by a relative error of at most 0.013.
Values may be sent and summed in bfloat16 or wider, within the bound.
No kernel may reach another device: no remote copies, remote signals or barrier semaphores. Data moves between devices by JAX's collectives and lax.ppermute only.
A program may use at most 192 MiB of HBM per device.

v0:
```python
import math

import jax
import jax.numpy as jnp
from jax import lax
from jax.sharding import PartitionSpec as P

HD = 128
STATE = 16
CONV = 4


NEG_FILL = -1e30


def prefix(shard, axis, join, neutral):
    place = lax.axis_index(axis)
    gathered = jax.tree.map(
        lambda a, kind: lax.all_gather(a.astype(kind), axis), shard, (jnp.bfloat16, jnp.bfloat16)
    )
    state = jax.tree.map(lambda a, e: jnp.zeros_like(a) + jnp.asarray(e, a.dtype), shard, neutral)

    def one(turn, state):
        return join(
            state,
            jax.tree.map(
                lambda a, own: lax.dynamic_index_in_dim(a, turn, 0, False).astype(own.dtype),
                gathered,
                shard,
            ),
        )

    return lax.fori_loop(0, place, one, state)


def passed_along(value, axis, steps):
    count = lax.axis_size(axis)
    first, last = (max(0, -steps), min(count, count - steps))
    return lax.ppermute(value, axis, [(source, source + steps) for source in range(first, last)])


def table_lookup(lookup_table, wanted):
    entries = lookup_table.shape[0]
    matches = wanted[:, None] == jnp.arange(entries, dtype=jnp.int32)[None, :]
    return jnp.sum(jnp.where(matches, lookup_table[None, :], 0), axis=1)


def attend(state, piece, context):
    queries4, query_pos, query_half, own_spans, mask_rows, span_order, half_rows = context
    key_piece, value_piece = piece
    piece_rows = key_piece.shape[0]
    row_ids = jnp.arange(piece_rows, dtype=jnp.int32)
    key_span = table_lookup(span_order, row_ids // half_rows)
    key_pos = key_span * half_rows + row_ids % half_rows
    entries = span_order.shape[0]
    picked = key_span[None, :, None] == jnp.arange(entries, dtype=jnp.int32)[None, None, :]
    granted = jnp.sum(jnp.where(picked, mask_rows[:, None, :], 0), axis=2)
    allowed = (granted == 1) | (key_span[None, :] == own_spans[:, None])
    allowed_rows = jnp.where(query_half[:, None] == 0, allowed[0][None, :], allowed[1][None, :])
    visible = allowed_rows & (key_pos[None, :] <= query_pos[:, None])
    local_kv = queries4.shape[1]
    key_split = key_piece.reshape(piece_rows, local_kv, HD)
    value_split = value_piece.reshape(piece_rows, local_kv, HD)
    scores = jnp.einsum(
        "rkgd,mkd->kgrm", queries4, key_split, preferred_element_type=jnp.float32
    ) * HD ** (-0.5)
    scores = jnp.where(visible[None, None], scores, NEG_FILL)
    running, totals, summed = state
    highest = jnp.maximum(running, jnp.max(scores, axis=3))
    weights = jnp.where(visible[None, None], jnp.exp(scores - highest[..., None]), 0.0)
    totals = jnp.sum(weights, axis=3)
    summed = jnp.einsum(
        "kgrm,mkd->kgrd",
        weights.astype(jnp.bfloat16),
        value_split,
        preferred_element_type=jnp.float32,
    )
    return (highest, totals, summed)


def attention(queries, key_heads, value_heads, span_order, block_mask):
    row_count = queries.shape[0]
    half_rows = row_count // 2
    head_devices = lax.axis_size("head")
    kv_count = key_heads.shape[1] // HD
    local_kv = max(1, kv_count // head_devices)
    query_local = queries.shape[1] // HD
    per_group = query_local // local_kv
    group_size = query_local * head_devices // kv_count
    kv_start = lax.axis_index("head") * query_local // group_size
    key_mine = lax.dynamic_slice_in_dim(key_heads, kv_start * HD, local_kv * HD, 1)
    value_mine = lax.dynamic_slice_in_dim(value_heads, kv_start * HD, local_kv * HD, 1)
    queries4 = queries.reshape(row_count, local_kv, per_group, HD)
    own_slot = lax.axis_index("ctx")
    own_spans = lax.dynamic_slice_in_dim(span_order, 2 * own_slot, 2)
    entries = span_order.shape[0]
    chosen = own_spans[:, None] == jnp.arange(entries, dtype=jnp.int32)[None, :]
    mask_rows = jnp.sum(jnp.where(chosen[:, :, None], block_mask[None], 0), axis=1)
    row_ids = jnp.arange(row_count, dtype=jnp.int32)
    query_half = row_ids // half_rows
    query_span = jnp.where(query_half == 0, own_spans[0], own_spans[1])
    query_pos = query_span * half_rows + row_ids % half_rows
    context = (queries4, query_pos, query_half, own_spans, mask_rows, span_order, half_rows)
    start_state = (
        jnp.full((local_kv, per_group, row_count), NEG_FILL, jnp.float32),
        jnp.zeros((local_kv, per_group, row_count), jnp.float32),
        jnp.zeros((local_kv, per_group, row_count, HD), jnp.float32),
    )
    highest, totals, summed = attend(
        start_state,
        (
            lax.all_gather(key_mine, "ctx", axis=0, tiled=True),
            lax.all_gather(value_mine, "ctx", axis=0, tiled=True),
        ),
        context,
    )
    result = summed / totals[..., None]
    return result.transpose(2, 0, 1, 3).reshape(row_count, -1).astype(jnp.bfloat16)


def link(earlier, later):
    return (earlier[0] * later[0], earlier[1] * later[0] + later[1])


def local_scan(step_dt, inputs_f, b_vals, c_vals, rate_table, carry_in, length):
    row_count, channels = step_dt.shape
    blocks = row_count // length
    decay_all = jnp.exp(step_dt[:, None, :] * rate_table[None])
    drive_all = (step_dt * inputs_f)[:, None, :] * b_vals[:, :, None]

    def one_block(state, packed):
        decay_block, drive_block, c_block = packed
        results = []
        for offset in range(length):
            state = decay_block[offset] * state + drive_block[offset]
            results.append(jnp.sum(state * c_block[offset][:, None], axis=0))
        return (state, jnp.stack(results, axis=0))

    packed = (
        decay_all.reshape(blocks, length, STATE, channels),
        drive_all.reshape(blocks, length, STATE, channels),
        c_vals.reshape(blocks, length, STATE),
    )
    last_state, outputs = lax.scan(one_block, carry_in, packed)
    return (last_state, outputs.reshape(row_count, channels))


def carry_across(through, own_end):
    return prefix(
        (through, own_end), "ctx", link, (jnp.ones_like(through), jnp.zeros_like(own_end))
    )[1]


def normalize(low_vals, low_gain):
    scale_inv = lax.rsqrt(jnp.mean(low_vals * low_vals, axis=1, keepdims=True) + 1e-06)
    return (low_vals * scale_inv * low_gain[None, :]).astype(jnp.bfloat16)


def mamba(
    mamba_in,
    gate_in,
    conv_weight,
    conv_bias,
    low_weight,
    bc_weight,
    low_gain,
    dt_weight,
    dt_bias,
    rate_log,
    skip_gain,
):
    row_count, channels = mamba_in.shape
    rim = passed_along(mamba_in[row_count - (CONV - 1) :], "ctx", 1)
    extended = jnp.concatenate([rim, mamba_in], axis=0)
    mixed = conv_bias[None, :] + sum(
        (
            conv_weight[offset][None, :] * extended[offset : offset + row_count].astype(jnp.float32)
            for offset in range(CONV)
        )
    )
    act_bf = jax.nn.silu(mixed).astype(jnp.bfloat16)
    low_part = jnp.dot(act_bf, low_weight, preferred_element_type=jnp.float32)
    bc_part = jnp.dot(act_bf, bc_weight, preferred_element_type=jnp.float32)
    low_sum, bc_sum = (
        lax.psum(low_part.astype(jnp.bfloat16), "head").astype(jnp.float32),
        lax.psum(bc_part.astype(jnp.bfloat16), "head").astype(jnp.float32),
    )
    normed = normalize(low_sum, low_gain)
    step_dt = jax.nn.softplus(
        jnp.dot(normed, dt_weight, preferred_element_type=jnp.float32) + dt_bias[None, :]
    )
    rate_table = -jnp.exp(rate_log).T
    inputs_f = act_bf.astype(jnp.float32)
    b_vals = bc_sum[:, :STATE]
    c_vals = bc_sum[:, STATE:]
    length = math.gcd(row_count, 32)
    empty = jnp.zeros((STATE, channels), jnp.float32)
    through = jnp.exp(rate_table * jnp.sum(step_dt, axis=0)[None, :])
    own_end = local_scan(step_dt, inputs_f, b_vals, c_vals, rate_table, empty, length)[0]
    entering = carry_across(through, own_end)
    outputs = local_scan(step_dt, inputs_f, b_vals, c_vals, rate_table, entering, length)[1]
    result = outputs + skip_gain[None, :] * inputs_f
    return (result * jax.nn.silu(gate_in.astype(jnp.float32))).astype(jnp.bfloat16)


def per_device(
    queries,
    key_heads,
    value_heads,
    span_order,
    block_mask,
    mamba_in,
    gate_in,
    conv_weight,
    conv_bias,
    low_weight,
    bc_weight,
    low_gain,
    dt_weight,
    dt_bias,
    rate_log,
    skip_gain,
):
    attn_out = attention(queries, key_heads, value_heads, span_order, block_mask)
    mamba_out = mamba(
        mamba_in,
        gate_in,
        conv_weight,
        conv_bias,
        low_weight,
        bc_weight,
        low_gain,
        dt_weight,
        dt_bias,
        rate_log,
        skip_gain,
    )
    return (attn_out, mamba_out)


def solution(mesh):
    in_specs = (
        P("ctx", "head"),
        P("ctx", None),
        P("ctx", None),
        P(),
        P(),
        P("ctx", "head"),
        P("ctx", "head"),
        P(None, "head"),
        P("head"),
        P("head", None),
        P("head", None),
        P(),
        P(None, "head"),
        P("head"),
        P("head", None),
        P("head"),
    )
    out_specs = (P("ctx", "head"), P("ctx", "head"))
    return jax.shard_map(
        per_device, mesh=mesh, in_specs=in_specs, out_specs=out_specs, check_vma=False
    )
```

profile of v0, /device:TPU:26, one launch (start us, length us, event | category | flops | bytes accessed | tf_op | source)
XLA Modules:
  0.0 294.0 jit_solution(15363560117941585995)
XLA Ops:
  15.6 3.5 %multiply_convert_fusion = bf16[128,4096]{1,0:T(8,128)(2,1)S(1)} fusion(bf16[128,4096]{1,0:T(8,128)(2,1)} %param.27, bf16[3,4096]{1,0:T(4,128)(2,1)S(1)} %collective-permute-done, f32[4096]{0:T(1024)S(1)} %bitcast.1187, f32[4096]{0:T(1024)S(1)} %bitcast.1188, f32[4096]{0:T(1024)S(1)} %bitcast.1186, f32[4096]{0:T(1024)S(1)} %bitcast.1185, f32[4096]{0:T(1024)} %param.30), kind=kLoop, calls=%fused_computation.376 | loop fusion | flops 13631488 | bytes 2203648 | tf_op jit(solution)/shard_map/convert_element_type | solution.py:181
  19.2 4.0 %convolution_convert_fusion = bf16[128,512]{1,0:T(8,128)(2,1)} fusion(bf16[128,4096]{1,0:T(8,128)(2,1)S(1)} %multiply_convert_fusion, bf16[4096,512]{1,0:T(8,128)(2,1)} %param.31), kind=kOutput, calls=%fused_computation.380 | convolution fusion | flops 536936448 | bytes 5373952 | tf_op jit(solution)/shard_map/dot_general | solution.py:182
  23.6 7.1 %psum.15 = bf16[128,32]{0,1:T(8,128)(2,1)S(1)} all-reduce(bf16[128,32]{0,1:T(8,128)(2,1)S(1)} %convolution_convert_fusion.1), channel_id=1, replica_groups=mesh['ctx'=8,'head'=4] {'head'}, use_global_device_ids=true, to_apply=%region_8.9 | all-reduce | flops 4096 | bytes 16384 | tf_op jit(solution)/shard_map/psum | solution.py:186
  30.9 26.4 %all-reduce.2.cloned.1.call-done = bf16[128,512]{1,0:T(8,128)(2,1)} async-done(((bf16[128,512]{1,0:T(8,128)(2,1)}), bf16[128,512]{1,0:T(8,128)(2,1)}) %all-reduce.2.cloned.1.call-update) | async-done | bytes 131088 | tf_op jit(solution)/shard_map/psum | solution.py:185
  58.3 4.3 %convert_multiply_fusion.3 = (f32[128,4096]{1,0:T(8,128)S(1)}, f32[4096]{0:T(1024)S(1)}, f32[128,4096]{1,0:T(8,128)S(1)}) fusion(bf16[128,4096]{1,0:T(8,128)(2,1)S(1)} %multiply_convert_fusion, f32[4096]{0:T(1024)S(1)} %copy-done.27, bf16[512,4096]{1,0:T(8,128)(2,1)} %param.34, bf16[128,512]{1,0:T(8,128)(2,1)} %all-reduce.2.cloned.1.call-done, ...), kind=kOutput, calls=%fused_computation.369 | convolution fusion | flops 542371840 | bytes 9603584 | tf_op jit(solution)/shard_map/dot_general | solution.py:190
  62.5 11.3 %broadcast_multiply_fusion = f32[4,32,16,4096]{3,2,1,0:T(8,128)} fusion(f32[4,32,16]{2,1,0:T(8,128)S(1)} %bitcast.1184, f32[4,32,4096]{2,1,0:T(8,128)S(1)} %bitcast.1144), kind=kLoop, calls=%fused_computation.356 | loop fusion | flops 8388608 | bytes 35659776 | tf_op jit(solution)/shard_map/mul | solution.py:129
  73.8 11.3 %multiply_exponential_fusion = f32[4,32,16,4096]{3,2,1,0:T(8,128)} fusion(f32[16,4096]{1,0:T(8,128)S(1)} %negate_bitcast_fusion, f32[4,32,4096]{2,1,0:T(8,128)S(1)} %bitcast.1143), kind=kLoop, calls=%fused_computation.355 | loop fusion | flops 8388608 | bytes 35913728 | tf_op jit(solution)/shard_map/exp | solution.py:128
  85.1 26.6 %while.37 = (s32[]{:T(128)}, f32[16,4096]{1,0:T(8,128)S(1)}, f32[4,32,16,4096]{3,2,1,0:T(8,128)}, f32[4,32,16,4096]{3,2,1,0:T(8,128)}, s32[]{:T(128)}, /*index=5...) while((s32[]{:T(128)}, f32[16,4096]{1,0:T(8,128)S(1)}, ...), condition=%wide.region_10.11_spmd.clone, body=%wide.region_9.10_spmd.clone.sunk | while | flops 4259874 | bytes 17302328 | solution.py:144
  85.1 6.6 %fusion.246 = f32[16,4096]{1,0:T(8,128)S(1)} fusion(f32[4,32,16,4096]{3,2,1,0:T(8,128)} %get-tuple-element.640, s32[]{:T(128)} %get-tuple-element.600, s32[]{:T(128)S(6)} %add.959, s32[]{:T(128)S(6)} %add.960, s32[]{:T(128)S(6)} %add.961, s32[]{:T(128)S(6)} %add.962, s32[]{:T(128)S(6)} %add.963, s32[]{:T(128)S(6)} %add.964, s32[]{:T(128)S(6)} %add.965, ...), kind=kLoop, calls=%fused_computation.228.clone.1 | loop fusion | flops 4259840 | bytes 17301632 | tf_op jit(solution)/shard_map/while/body/eval_jaxpr/add | solution.py:135
  91.8 6.6 %fusion.246 = f32[16,4096]{1,0:T(8,128)S(1)} fusion(f32[4,32,16,4096]{3,2,1,0:T(8,128)} %get-tuple-element.640, s32[]{:T(128)} %get-tuple-element.600, s32[]{:T(128)S(6)} %add.959, s32[]{:T(128)S(6)} %add.960, s32[]{:T(128)S(6)} %add.961, s32[]{:T(128)S(6)} %add.962, s32[]{:T(128)S(6)} %add.963, s32[]{:T(128)S(6)} %add.964, s32[]{:T(128)S(6)} %add.965, ...), kind=kLoop, calls=%fused_computation.228.clone.1 | loop fusion | flops 4259840 | bytes 17301632 | tf_op jit(solution)/shard_map/while/body/eval_jaxpr/add | solution.py:135
  98.4 6.6 %fusion.246 = f32[16,4096]{1,0:T(8,128)S(1)} fusion(f32[4,32,16,4096]{3,2,1,0:T(8,128)} %get-tuple-element.640, s32[]{:T(128)} %get-tuple-element.600, s32[]{:T(128)S(6)} %add.959, s32[]{:T(128)S(6)} %add.960, s32[]{:T(128)S(6)} %add.961, s32[]{:T(128)S(6)} %add.962, s32[]{:T(128)S(6)} %add.963, s32[]{:T(128)S(6)} %add.964, s32[]{:T(128)S(6)} %add.965, ...), kind=kLoop, calls=%fused_computation.228.clone.1 | loop fusion | flops 4259840 | bytes 17301632 | tf_op jit(solution)/shard_map/while/body/eval_jaxpr/add | solution.py:135
  105.1 6.6 %fusion.246 = f32[16,4096]{1,0:T(8,128)S(1)} fusion(f32[4,32,16,4096]{3,2,1,0:T(8,128)} %get-tuple-element.640, s32[]{:T(128)} %get-tuple-element.600, s32[]{:T(128)S(6)} %add.959, s32[]{:T(128)S(6)} %add.960, s32[]{:T(128)S(6)} %add.961, s32[]{:T(128)S(6)} %add.962, s32[]{:T(128)S(6)} %add.963, s32[]{:T(128)S(6)} %add.964, s32[]{:T(128)S(6)} %add.965, ...), kind=kLoop, calls=%fused_computation.228.clone.1 | loop fusion | flops 4259840 | bytes 17301632 | tf_op jit(solution)/shard_map/while/body/eval_jaxpr/add | solution.py:135
  114.9 26.7 %all_gather.18 = bf16[1024,256]{0,1:T(8,128)(2,1)S(1)} all-gather(bf16[128,256]{0,1:T(8,128)(2,1)S(1)} %copy.47), channel_id=1, replica_groups=mesh['ctx'=8,'head'=4] {'ctx'}, dimensions={0}, use_global_device_ids=true | all-gather | bytes 589824 | tf_op jit(solution)/shard_map/all_gather | solution.py:112
  141.6 4.7 %fusion.160 = (f32[2,8,128]{2,1,0:T(8,128)S(1)}, f32[2,1024,128,8]{2,1,3,0:T(8,128)}) fusion(pred[128,1024]{0,1:T(8,128)(4,1)S(1)} %compare_and_fusion, bf16[1024,2,128,1]{0,2,3,1:T(8,128)(2,1)S(1)} %bitcast.1146, bf16[128,2,8,128]{3,2,1,0:T(8,128)(2,1)S(1)} %bitcast.1145), kind=kOutput, calls=%fused_computation.359 | convolution fusion | flops 543160320 | bytes 9576448 | tf_op jit(solution)/shard_map/rkgd,mkd->kgrm/dot_general | solution.py:64
  147.0 31.7 %all_gather.19 = bf16[1024,256]{1,0:T(8,128)(2,1)S(1)} all-gather(bf16[128,256]{1,0:T(8,128)(2,1)S(1)} %constant_dynamic-slice_fusion.32), channel_id=1, replica_groups=mesh['ctx'=8,'head'=4] {'ctx'}, dimensions={0}, use_global_device_ids=true | all-gather | bytes 589824 | tf_op jit(solution)/shard_map/all_gather | solution.py:113
  178.9 4.7 %fusion.161 = f32[2,8,128]{2,1,0:T(8,128)S(1)} fusion(f32[2,1024,128,8]{2,1,3,0:T(8,128)} %get-tuple-element.279, f32[2,8,128]{2,1,0:T(8,128)S(1)} %broadcast_maximum_fusion, pred[128,1024]{0,1:T(8,128)(4,1)S(1)} %compare_and_fusion), kind=kLoop, calls=%fused_computation.361 | loop fusion | flops 10483712 | bytes 8536064 | tf_op jit(solution)/shard_map/reduce_sum | solution.py:71
  188.8 5.2 %all-gather.5.cloned.1.call-done = bf16[128,4096]{1,0:T(8,128)(2,1)} async-done(((bf16[16,4096]{1,0:T(8,128)(2,1)}), bf16[128,4096]{1,0:T(8,128)(2,1)}) %all-gather.5.cloned.1.call-update) | async-done | bytes 1048592 | tf_op jit(solution)/shard_map/all_gather | solution.py:19
  194.0 7.6 %while.35 = (s32[]{:T(128)}, f32[16,4096]{1,0:T(8,128)S(1)}, s32[]{:T(128)}, bf16[8,16,4096]{2,1,0:T(8,128)(2,1)}, bf16[8,16,4096]{2,1,0:T(8,128)(2,1)}, /*index=5*/s32[]{:T(128)}, s32[]{:T(128)}, s32[]{:T(128)}) while((s32[]{:T(128)}, f32[16,4096]{1,0:T(8,128)S(1)}, s32[]{:T(128)}, bf16[8,16,4096]{2,1,0:T(8,128)(2,1)}, ...), condition=%wide.region_12.13_spmd, body=%wide.region_11.12_spmd.sunk | while | flops 262149 | bytes 786555 | solution.py:33
  201.6 81.9 %while.36 = (s32[]{:T(128)}, f32[16,4096]{1,0:T(8,128)S(1)}, f32[4,32,4096]{2,1,0:T(8,128)}, f32[4,32,16,4096]{3,2,1,0:T(8,128)}, f32[4,32,16,4096]{3,2,1,0:T(8,...) while((s32[]{:T(128)}, f32[16,4096]{1,0:T(8,128)S(1)}, ...), condition=%wide.region_46.47_spmd, body=%wide.region_13.46_spmd.sunk | while | flops 8388641 | bytes 36451320 | solution.py:144
  206.1 7.9 %multiply_reduce_fusion.49 = (f32[4096]{0:T(1024)S(1)}, f32[16,4096]{1,0:T(8,128)S(1)}, f32[16,4096]{1,0:T(8,128)}, f32[16,4096]{1,0:T(8,128)}, f32[16,4096]{1,0...) fusion(f32[16]{0:T(128)S(1)} %get-tuple-element.465, ...), kind=kLoop, calls=%fused_computation.131.clone.1 | loop fusion | flops 4321280 | bytes 25182400 | tf_op jit(solution)/shard_map/while/body/eval_jaxpr/reduce_sum | solution.py:136
  226.5 7.9 %multiply_reduce_fusion.49 = (f32[4096]{0:T(1024)S(1)}, f32[16,4096]{1,0:T(8,128)S(1)}, f32[16,4096]{1,0:T(8,128)}, f32[16,4096]{1,0:T(8,128)}, f32[16,4096]{1,0...) fusion(f32[16]{0:T(128)S(1)} %get-tuple-element.465, ...), kind=kLoop, calls=%fused_computation.131.clone.1 | loop fusion | flops 4321280 | bytes 25182400 | tf_op jit(solution)/shard_map/while/body/eval_jaxpr/reduce_sum | solution.py:136
  247.0 7.9 %multiply_reduce_fusion.49 = (f32[4096]{0:T(1024)S(1)}, f32[16,4096]{1,0:T(8,128)S(1)}, f32[16,4096]{1,0:T(8,128)}, f32[16,4096]{1,0:T(8,128)}, f32[16,4096]{1,0...) fusion(f32[16]{0:T(128)S(1)} %get-tuple-element.465, ...), kind=kLoop, calls=%fused_computation.131.clone.1 | loop fusion | flops 4321280 | bytes 25182400 | tf_op jit(solution)/shard_map/while/body/eval_jaxpr/reduce_sum | solution.py:136
  267.4 7.9 %multiply_reduce_fusion.49 = (f32[4096]{0:T(1024)S(1)}, f32[16,4096]{1,0:T(8,128)S(1)}, f32[16,4096]{1,0:T(8,128)}, f32[16,4096]{1,0:T(8,128)}, f32[16,4096]{1,0...) fusion(f32[16]{0:T(128)S(1)} %get-tuple-element.465, ...), kind=kLoop, calls=%fused_computation.131.clone.1 | loop fusion | flops 4321280 | bytes 25182400 | tf_op jit(solution)/shard_map/while/body/eval_jaxpr/reduce_sum | solution.py:136
  283.5 4.0 %fusion.168 = bf16[128,4096]{1,0:T(8,128)(2,1)} fusion(bf16[128,4096]{1,0:T(8,128)(2,1)} %copy-done.3, bf16[128,4096]{1,0:T(8,128)(2,1)} %param.28, f32[4,32,4096]{2,1,0:T(8,128)} %get-tuple-element.102, f32[4096]{0:T(1024)} %param.37), kind=kLoop, calls=%fused_computation.372 | loop fusion | flops 5242880 | bytes 5259264 | tf_op jit(solution)/shard_map/convert_element_type | solution.py:203
  (310 shorter events, 75.4 us)
Async XLA Ops:
  7.2 7.5 %copy-start = (bf16[128,1024]{1,0:T(8,128)(2,1)S(1)}, bf16[128,1024]{1,0:T(8,128)(2,1)}, u32[]{:S(2)}) copy-start(bf16[128,1024]{1,0:T(8,128)(2,1)} %param.23) | copy-start | bytes 786436
  7.2 50.0 %all-reduce.2.cloned.1.call-start = ((), (), s32[]{:S(2)}) async-start(), calls=%async_computation | async-start | bytes 262144 | tf_op jit(solution)/shard_map/psum | solution.py:185
  8.1 7.5 %collective-permute-start = (bf16[3,4096]{1,0:T(4,128)(2,1)S(1)}, bf16[3,4096]{1,0:T(4,128)(2,1)S(1)}, u32[]{:S(2)}, u32[]{:S(2)}) collective-permute-start(bf16[3,4096]{1,0:T(4,128)(2,1)S(1)} %slice.693), channel_id=1, source_target_pairs={{0,4},{4,8},{8,12},{12,16},{16,20},{20,24},{24,28},{1,5},{5,9},{9,... | collective-permute-start | bytes 73736 | tf_op jit(solution)/shard_map/ppermute | solution.py:39
  19.1 39.1 %copy-start.3 = (bf16[128,4096]{1,0:T(8,128)(2,1)}, bf16[128,4096]{1,0:T(8,128)(2,1)S(1)}, u32[]{:S(2)}) copy-start(bf16[128,4096]{1,0:T(8,128)(2,1)S(1)} %multiply_convert_fusion) | copy-start | bytes 3145732
  19.1 39.1 %copy-start.27 = (f32[4096]{0:T(1024)S(1)}, f32[4096]{0:T(1024)}, u32[]{:S(2)}) copy-start(f32[4096]{0:T(1024)} %param.35) | copy-start | bytes 49156
  19.1 39.1 %copy-start.28 = (f32[512]{0:T(512)S(1)}, f32[512]{0:T(512)}, u32[]{:S(2)}) copy-start(f32[512]{0:T(512)} %param.33) | copy-start | bytes 6148
  23.1 165.6 %all-gather.7.cloned.1.call-start = ((), (), s32[]{:S(2)}) async-start(), calls=%async_computation.2 | async-start | bytes 1179648 | tf_op jit(solution)/shard_map/all_gather | solution.py:19
  85.1 28.7 %copy-start.5 = (bf16[128,2048]{1,0:T(8,128)(2,1)S(1)}, bf16[128,2048]{1,0:T(8,128)(2,1)}, u32[]{:S(2)}) copy-start(bf16[128,2048]{1,0:T(8,128)(2,1)} %param.22) | copy-start | bytes 1572868
  112.4 81.5 %all-gather.5.cloned.1.call-start = ((), (), s32[]{:S(2)}) async-start(), calls=%async_computation.1 | async-start | bytes 1179648 | tf_op jit(solution)/shard_map/all_gather | solution.py:19
  178.9 6.0 %copy-start.2 = (f32[2,1024,128,8]{2,1,3,0:T(8,128)S(1)}, f32[2,1024,128,8]{2,1,3,0:T(8,128)}, u32[]{:S(2)}) copy-start(f32[2,1024,128,8]{2,1,3,0:T(8,128)} %get-tuple-element.279) | copy-start | bytes 25165828
  214.0 4.7 %copy-start.10 = (f32[16]{0:T(128)S(1)}, f32[16]{0:T(128)}, u32[]{:S(2)}) copy-start(f32[16]{0:T(128)} %get-tuple-element.523) | copy-start | bytes 196 | tf_op jit(solution)/shard_map/while
  214.0 4.7 %copy-start.11 = (f32[16]{0:T(128)S(1)}, f32[16]{0:T(128)}, u32[]{:S(2)}) copy-start(f32[16]{0:T(128)} %get-tuple-element.525) | copy-start | bytes 196 | tf_op jit(solution)/shard_map/while
  214.0 4.9 %copy-start.8 = (f32[16]{0:T(128)S(1)}, f32[16]{0:T(128)}, u32[]{:S(2)}) copy-start(f32[16]{0:T(128)} %get-tuple-element.517) | copy-start | bytes 196 | tf_op jit(solution)/shard_map/while
  214.0 4.9 %copy-start.9 = (f32[16]{0:T(128)S(1)}, f32[16]{0:T(128)}, u32[]{:S(2)}) copy-start(f32[16]{0:T(128)} %get-tuple-element.519) | copy-start | bytes 196 | tf_op jit(solution)/shard_map/while
  214.0 5.0 %copy-start.7 = (f32[16]{0:T(128)S(1)}, f32[16]{0:T(128)}, u32[]{:S(2)}) copy-start(f32[16]{0:T(128)} %get-tuple-element.513) | copy-start | bytes 196 | tf_op jit(solution)/shard_map/while
  234.5 4.9 %copy-start.8 = (f32[16]{0:T(128)S(1)}, f32[16]{0:T(128)}, u32[]{:S(2)}) copy-start(f32[16]{0:T(128)} %get-tuple-element.517) | copy-start | bytes 196 | tf_op jit(solution)/shard_map/while
  234.5 4.9 %copy-start.9 = (f32[16]{0:T(128)S(1)}, f32[16]{0:T(128)}, u32[]{:S(2)}) copy-start(f32[16]{0:T(128)} %get-tuple-element.519) | copy-start | bytes 196 | tf_op jit(solution)/shard_map/while
  234.5 5.0 %copy-start.7 = (f32[16]{0:T(128)S(1)}, f32[16]{0:T(128)}, u32[]{:S(2)}) copy-start(f32[16]{0:T(128)} %get-tuple-element.513) | copy-start | bytes 196 | tf_op jit(solution)/shard_map/while
  255.0 4.9 %copy-start.8 = (f32[16]{0:T(128)S(1)}, f32[16]{0:T(128)}, u32[]{:S(2)}) copy-start(f32[16]{0:T(128)} %get-tuple-element.517) | copy-start | bytes 196 | tf_op jit(solution)/shard_map/while
  255.0 4.9 %copy-start.9 = (f32[16]{0:T(128)S(1)}, f32[16]{0:T(128)}, u32[]{:S(2)}) copy-start(f32[16]{0:T(128)} %get-tuple-element.519) | copy-start | bytes 196 | tf_op jit(solution)/shard_map/while
  255.0 5.0 %copy-start.7 = (f32[16]{0:T(128)S(1)}, f32[16]{0:T(128)}, u32[]{:S(2)}) copy-start(f32[16]{0:T(128)} %get-tuple-element.513) | copy-start | bytes 196 | tf_op jit(solution)/shard_map/while
  275.4 4.9 %copy-start.8 = (f32[16]{0:T(128)S(1)}, f32[16]{0:T(128)}, u32[]{:S(2)}) copy-start(f32[16]{0:T(128)} %get-tuple-element.517) | copy-start | bytes 196 | tf_op jit(solution)/shard_map/while
  275.4 4.9 %copy-start.9 = (f32[16]{0:T(128)S(1)}, f32[16]{0:T(128)}, u32[]{:S(2)}) copy-start(f32[16]{0:T(128)} %get-tuple-element.519) | copy-start | bytes 196 | tf_op jit(solution)/shard_map/while
  275.4 5.0 %copy-start.7 = (f32[16]{0:T(128)S(1)}, f32[16]{0:T(128)}, u32[]{:S(2)}) copy-start(f32[16]{0:T(128)} %get-tuple-element.513) | copy-start | bytes 196 | tf_op jit(solution)/shard_map/while
  (69 other events, 184.6 us)
Sparse Core Ops, SparseCore 0:
  23.3 33.9 all-reduce.1
  112.6 39.1 all-gather.6
  153.9 39.9 all-gather.4
where the time goes:
time: 295 us; the launch traced here: 294 us
  other arithmetic  137 us (46%)
  blocking collectives  65.5 us (22%)
  waiting for transfers between devices  31.6 us (11%)
  local copies, waits for them, and re-layouts  27.7 us (9%)
  matrix products  15.5 us (5%)
  between operations  14.1 us (5%)
    reduce_sum x68, other arithmetic, one_block(): results.append(jnp.sum(state * c_block[offset][:, None], axis=0))  60.4 us
    all_gather x1, blocking collectives, attention(): lax.all_gather(value_mine, 'ctx', axis=0, tiled=True)  31.7 us
    all_gather x1, blocking collectives, attention(): lax.all_gather(key_mine, 'ctx', axis=0, tiled=True)  26.7 us
    add x4, other arithmetic, one_block(): state = decay_block[offset] * state + drive_block[offset]  26.5 us
    psum x1, waiting for transfers between devices, mamba(): lax.psum(low_part.astype(jnp.bfloat16), 'head').astype(jnp.float32)  26.4 us
    mul x8, local copies, waits for them, and re-layouts, one_block(): results.append(jnp.sum(state * c_block[offset][:, None], axis=0))  13.1 us
    exp x1, other arithmetic, local_scan(): decay_all = jnp.exp(step_dt[:, None, :] * rate_table[None])  11.3 us
    mul x1, other arithmetic, local_scan(): drive_all = (step_dt * inputs_f)[:, None, :] * b_vals[:, :, None]  11.3 us
  transfers between devices with their start and end apart: 4, of which 2 were waited for; matrix products, arithmetic and copies ran while one was open for 8% of the time, Pallas kernels for 0%

commit v1 on v0

v1 whole, which is shorter than its diff:
```python
import functools

import jax
import jax.numpy as jnp
from jax import lax
from jax.experimental import pallas as pl
from jax.experimental.pallas import tpu as pltpu
from jax.sharding import PartitionSpec as P

HD = 128
STATE = 16
CONV = 4
RIM = 8
LANES = 128
TOKEN_BLOCK = 16
LOG2E = 1.4426950408889634
NEG_FILL = -1e30
F32 = jnp.float32
BF16 = jnp.bfloat16


def swap(value, axis, step):
    count = lax.axis_size(axis)
    return lax.ppermute(value, axis, [(i, i ^ step) for i in range(count)])


def bits_of(count):
    steps = []
    while 2 ** len(steps) < count:
        steps.append(2 ** len(steps))
    return steps


def cost(flops, moved, exps=0):
    return pl.CostEstimate(flops=flops, bytes_accessed=moved, transcendentals=exps)


def attention_body(
    place, span_order, block_mask, q_ref, ka_ref, kb_ref, va_ref, vb_ref, out_ref, bias, *, order, heads
):
    half = q_ref.shape[0] // 2
    rows = 2 * half
    side = ka_ref.shape[0]

    @pl.when(pl.program_id(0) == 0)
    def _():
        me = place[0]
        row = lax.broadcasted_iota(jnp.int32, (half, rows), 0)
        col = lax.broadcasted_iota(jnp.int32, (half, rows), 1)
        lead = jnp.where(col < half, col, col - half) - row
        for query_half in range(2):
            query_span = span_order[2 * me + query_half]
            for piece, flip in enumerate(order):
                reach = []
                for key_half in range(2):
                    key_span = span_order[2 * (me ^ flip) + key_half]
                    granted = (block_mask[query_span, key_span] == 1) | (query_span == key_span)
                    reach.append(jnp.where(granted, (query_span - key_span) * half, -rows))
                limit = jnp.where(col < half, reach[0], reach[1])
                bias[query_half * half : (query_half + 1) * half, piece * rows : (piece + 1) * rows] = (
                    jnp.where(lead <= limit, 0.0, NEG_FILL)
                )

    contract = (((1,), (1,)), ((), ()))
    scale = HD ** (-0.5) * LOG2E
    for head in range(heads):
        cols = slice(head * HD, (head + 1) * HD)
        query = q_ref[:, cols]
        first = lax.dot_general(query, ka_ref[...], contract, preferred_element_type=F32)
        second = lax.dot_general(query, kb_ref[...], contract, preferred_element_type=F32)
        first = first * scale + bias[:, :side]
        second = second * scale + bias[:, side:]
        top = jnp.maximum(
            jnp.max(first, axis=1, keepdims=True), jnp.max(second, axis=1, keepdims=True)
        )
        first = jnp.exp2(first - top)
        second = jnp.exp2(second - top)
        total = jnp.sum(first, axis=1, keepdims=True) + jnp.sum(second, axis=1, keepdims=True)
        summed = jnp.dot(first.astype(BF16), va_ref[...], preferred_element_type=F32)
        summed = summed + jnp.dot(second.astype(BF16), vb_ref[...], preferred_element_type=F32)
        out_ref[:, cols] = (summed / total).astype(BF16)


def attention_call(place, span_order, block_mask, queries, near, far, order):
    rows, width = queries.shape
    local_kv = near.shape[1] // (2 * HD)
    heads = width // HD // local_kv
    side = near.shape[0]
    smem = pl.BlockSpec(memory_space=pltpu.SMEM)
    keys = pl.BlockSpec((side, HD), lambda g: (0, g))
    values = pl.BlockSpec((side, HD), lambda g: (0, local_kv + g))
    wide = pl.BlockSpec((rows, heads * HD), lambda g: (0, g))
    entries = rows * 2 * side * local_kv * heads
    return pl.pallas_call(
        functools.partial(attention_body, order=order, heads=heads),
        grid=(local_kv,),
        in_specs=[smem, smem, smem, wide, keys, keys, values, values],
        out_specs=wide,
        out_shape=jax.ShapeDtypeStruct((rows, width), BF16),
        scratch_shapes=[pltpu.VMEM((rows, 2 * side), F32)],
        cost_estimate=cost(entries * HD * 4, 4 * rows * width + 8 * side * local_kv * HD, entries),
        name="attention",
    )(place, span_order, block_mask, queries, near, far, near, far)


def front_body(x_ref, rim_ref, weight_ref, bias_ref, low_ref, bc_ref, act_ref, part_ref, low_sum, bc_sum):
    step = pl.program_id(0)
    rows = x_ref.shape[0]
    rank = low_ref.shape[1]
    extended = jnp.concatenate([rim_ref[...].astype(F32), x_ref[...].astype(F32)], axis=0)
    mixed = bias_ref[...]
    for tap in range(CONV):
        start = RIM - (CONV - 1) + tap
        mixed = mixed + weight_ref[tap : tap + 1, :] * extended[start : start + rows, :]
    act = (mixed / (1.0 + jnp.exp(-mixed))).astype(BF16)
    act_ref[...] = act
    low = jnp.dot(act, low_ref[...], preferred_element_type=F32)
    bc = jnp.dot(act, bc_ref[...], preferred_element_type=F32)

    @pl.when(step == 0)
    def _():
        low_sum[...] = low
        bc_sum[...] = bc

    @pl.when(step > 0)
    def _():
        low_sum[...] += low
        bc_sum[...] += bc

    @pl.when(step == pl.num_programs(0) - 1)
    def _():
        part_ref[:, :rank] = low_sum[...].astype(BF16)
        part_ref[:, rank:] = bc_sum[...].astype(BF16)


def front_call(mamba_in, rim, conv_weight, conv_bias, low_weight, bc_weight):
    rows, channels = mamba_in.shape
    rank, maps = low_weight.shape[1], bc_weight.shape[1]
    width = min(512, channels)
    block = pl.BlockSpec((rows, width), lambda i: (0, i))
    return pl.pallas_call(
        front_body,
        grid=(channels // width,),
        in_specs=[
            block,
            pl.BlockSpec((RIM, width), lambda i: (0, i)),
            pl.BlockSpec((CONV, width), lambda i: (0, i)),
            pl.BlockSpec((1, width), lambda i: (0, i)),
            pl.BlockSpec((width, rank), lambda i: (i, 0)),
            pl.BlockSpec((width, maps), lambda i: (i, 0)),
        ],
        out_specs=[block, pl.BlockSpec((rows, rank + maps), lambda i: (0, 0))],
        out_shape=[
            jax.ShapeDtypeStruct((rows, channels), BF16),
            jax.ShapeDtypeStruct((rows, rank + maps), BF16),
        ],
        scratch_shapes=[pltpu.VMEM((rows, rank), F32), pltpu.VMEM((rows, maps), F32)],
        cost_estimate=cost(
            2 * rows * channels * (rank + maps), channels * (4 * rows + 2 * (rank + maps)), rows * channels
        ),
        name="front",
    )(mamba_in, rim, conv_weight, conv_bias, low_weight, bc_weight)


def spread_rows(table, spread):
    rows = table.shape[0]
    tall = rows * STATE
    picker = lax.broadcasted_iota(jnp.int32, (tall, rows), 0) // STATE
    picker = picker == lax.broadcasted_iota(jnp.int32, (tall, rows), 1)
    picked = jnp.dot(
        picker.astype(F32).astype(BF16), table.astype(BF16), preferred_element_type=F32
    )
    state = lax.broadcasted_iota(jnp.int32, (tall, STATE), 0) % STATE
    kept = state == lax.broadcasted_iota(jnp.int32, (tall, STATE), 1)
    picked = jnp.where(kept, picked, 0.0).astype(BF16)
    spread[...] = jnp.dot(picked, jnp.ones((STATE, LANES), BF16), preferred_element_type=F32)


def advance(states, tiles, rates, step_ref, drive_ref, spread, base, offset):
    start = pl.multiple_of(base, TOKEN_BLOCK)
    inmap = spread[pl.ds(start * STATE + offset * STATE, STATE), :]
    moved = []
    for tile in range(tiles):
        lanes = pl.ds(tile * LANES, LANES)
        step = step_ref.at[pl.ds(start, TOKEN_BLOCK), lanes][pl.ds(offset, 1), :]
        drive = drive_ref.at[pl.ds(start, TOKEN_BLOCK), lanes][pl.ds(offset, 1), :]
        moved.append(jnp.exp2(step * rates[tile]) * states[tile] + drive * inmap)
    return moved


def softplus(v):
    small = jnp.exp(-jnp.abs(v))
    return jnp.maximum(v, 0.0) + jnp.log1p(small)


def ends_body(
    mine_ref, other_ref, gain_ref, weight_ref, bias_ref, rate_ref, act_ref, step_ref, end_ref, bc_ref, normed, spread, drive
):
    rows, width = act_ref.shape
    rank = gain_ref.shape[1]
    tiles = width // LANES

    @pl.when(pl.program_id(0) == 0)
    def _():
        low = mine_ref[:, :rank].astype(F32) + other_ref[:, :rank].astype(F32)
        scale = lax.rsqrt(jnp.mean(low * low, axis=1, keepdims=True) + 1e-06)
        normed[...] = (low * scale * gain_ref[...]).astype(BF16)
        bc = mine_ref[:, rank:].astype(F32) + other_ref[:, rank:].astype(F32)
        bc_ref[...] = bc
        spread_rows(bc[:, :STATE], spread)

    step = softplus(
        jnp.dot(normed[...], weight_ref[...], preferred_element_type=F32) + bias_ref[...]
    )
    step_ref[...] = step
    drive[...] = step * act_ref[...].astype(F32)
    end_ref[STATE:, :] = jnp.sum(step, axis=0, keepdims=True).astype(BF16)
    rates = [rate_ref[:, tile * LANES : (tile + 1) * LANES] for tile in range(tiles)]

    def block(index, states):
        states = list(states)
        for offset in range(TOKEN_BLOCK):
            states = advance(
                states, tiles, rates, step_ref, drive, spread, index * TOKEN_BLOCK, offset
            )
        return tuple(states)

    states = lax.fori_loop(
        0, rows // TOKEN_BLOCK, block, tuple(jnp.zeros((STATE, LANES), F32) for _ in range(tiles))
    )
    for tile in range(tiles):
        end_ref[:STATE, tile * LANES : (tile + 1) * LANES] = states[tile].astype(BF16)


def ends_call(mine, other, low_gain, dt_weight, dt_bias, rates, act):
    rows, channels = act.shape
    rank = dt_weight.shape[0]
    both = mine.shape[1]
    width = min(1024, channels)
    block = pl.BlockSpec((rows, width), lambda i: (0, i))
    whole = lambda shape: pl.BlockSpec(shape, lambda i: (0, 0))
    return pl.pallas_call(
        ends_body,
        grid=(channels // width,),
        in_specs=[
            whole((rows, both)),
            whole((rows, both)),
            whole((1, rank)),
            pl.BlockSpec((rank, width), lambda i: (0, i)),
            pl.BlockSpec((1, width), lambda i: (0, i)),
            pl.BlockSpec((STATE, width), lambda i: (0, i)),
            block,
        ],
        out_specs=[
            block,
            pl.BlockSpec((STATE + 1, width), lambda i: (0, i)),
            whole((rows, both - rank)),
        ],
        out_shape=[
            jax.ShapeDtypeStruct((rows, channels), F32),
            jax.ShapeDtypeStruct((STATE + 1, channels), BF16),
            jax.ShapeDtypeStruct((rows, both - rank), F32),
        ],
        scratch_shapes=[
            pltpu.VMEM((rows, rank), BF16),
            pltpu.VMEM((rows * STATE, LANES), F32),
            pltpu.VMEM((rows, width), F32),
        ],
        cost_estimate=cost(
            channels * rows * (2 * rank + 4 * STATE), channels * (6 * rows + 2 * rank), rows * channels * STATE
        ),
        name="ends",
    )(mine, other, low_gain, dt_weight, dt_bias, rates, act)


def scan_body(
    step_ref, act_ref, gate_ref, bc_ref, rate_ref, enter_ref, skip_ref, out_ref, spread, outmap, drive, even, odd
):
    rows, width = act_ref.shape
    tiles = width // LANES
    deep = TOKEN_BLOCK * STATE

    @pl.when(pl.program_id(0) == 0)
    def _():
        spread_rows(bc_ref[:, :STATE], spread)
        place = lax.broadcasted_iota(jnp.int32, (STATE, deep), 1)
        repeat = (place % STATE) == lax.broadcasted_iota(jnp.int32, (STATE, deep), 0)
        wide = jnp.dot(
            bc_ref[:, STATE:].astype(BF16), repeat.astype(F32).astype(BF16), preferred_element_type=F32
        )
        token = lax.broadcasted_iota(jnp.int32, (rows, deep), 0) % TOKEN_BLOCK
        own = token == lax.broadcasted_iota(jnp.int32, (rows, deep), 1) // STATE
        outmap[...] = jnp.where(own, wide, 0.0).astype(BF16)

    drive[...] = step_ref[...] * act_ref[...].astype(F32)
    rates = [rate_ref[:, tile * LANES : (tile + 1) * LANES] for tile in range(tiles)]

    def walk(index, states, held):
        states = list(states)
        for offset in range(TOKEN_BLOCK):
            states = advance(
                states, tiles, rates, step_ref, drive, spread, index * TOKEN_BLOCK, offset
            )
            for tile in range(tiles):
                held[offset * STATE : (offset + 1) * STATE, tile * LANES : (tile + 1) * LANES] = states[tile]
        return tuple(states)

    def emit(index, held):
        span = pl.ds(pl.multiple_of(index * TOKEN_BLOCK, TOKEN_BLOCK), TOKEN_BLOCK)
        summed = jnp.dot(outmap[span, :], held[...].astype(BF16), preferred_element_type=F32)
        summed = summed + skip_ref[...] * act_ref[span, :].astype(F32)
        gate = gate_ref[span, :].astype(F32)
        out_ref[span, :] = (summed * (gate / (1.0 + jnp.exp(-gate)))).astype(BF16)

    def pair(index, states):
        states = walk(2 * index + 1, states, odd)
        emit(2 * index, even)
        states = walk(2 * index + 2, states, even)
        emit(2 * index + 1, odd)
        return states

    blocks = rows // TOKEN_BLOCK
    states = tuple(enter_ref[:, tile * LANES : (tile + 1) * LANES] for tile in range(tiles))
    states = walk(0, states, even)
    states = lax.fori_loop(0, blocks // 2 - 1, pair, states)
    walk(blocks - 1, states, odd)
    emit(blocks - 2, even)
    emit(blocks - 1, odd)


def scan_call(step, act, gate, bc, rates, enter, skip):
    rows, channels = act.shape
    width = min(1024, channels)
    block = pl.BlockSpec((rows, width), lambda i: (0, i))
    table = pl.BlockSpec((STATE, width), lambda i: (0, i))
    deep = TOKEN_BLOCK * STATE
    return pl.pallas_call(
        scan_body,
        grid=(channels // width,),
        in_specs=[
            block,
            block,
            block,
            pl.BlockSpec(bc.shape, lambda i: (0, 0)),
            table,
            table,
            pl.BlockSpec((1, width), lambda i: (0, i)),
        ],
        out_specs=block,
        out_shape=jax.ShapeDtypeStruct((rows, channels), BF16),
        scratch_shapes=[
            pltpu.VMEM((rows * STATE, LANES), F32),
            pltpu.VMEM((rows, deep), BF16),
            pltpu.VMEM((rows, width), F32),
            pltpu.VMEM((deep, width), F32),
            pltpu.VMEM((deep, width), F32),
        ],
        cost_estimate=cost(8 * channels * rows * STATE, channels * rows * 10, rows * channels * STATE),
        name="scan",
    )(step, act, gate, bc, rates, enter, skip)


def entering(ends, rates):
    place = lax.axis_index("ctx")
    count = lax.axis_size("ctx")
    total = (ends[STATE:].astype(F32), ends[:STATE].astype(F32))
    before = tuple(jnp.zeros_like(part) for part in total)

    def join(early, late):
        return (early[0] + late[0], early[1] * jnp.exp2(rates * late[0]) + late[1])

    packed = ends
    for step in bits_of(count):
        last = 2 * step == count
        if last:
            got = lax.ppermute(packed, "ctx", [(i, i ^ step) for i in range(count) if not i & step])
        else:
            got = swap(packed, "ctx", step)
        got = (got[STATE:].astype(F32), got[:STATE].astype(F32))
        upper = (place & step) != 0
        joined = join(got, before)
        before = tuple(jnp.where(upper, new, old) for new, old in zip(joined, before))
        if not last:
            above, below = join(got, total), join(total, got)
            total = tuple(jnp.where(upper, a, b) for a, b in zip(above, below))
            packed = jnp.concatenate([total[1], total[0]], axis=0).astype(BF16)
    return before[1]


def per_device(
    queries,
    key_heads,
    value_heads,
    span_order,
    block_mask,
    mamba_in,
    gate_in,
    conv_weight,
    conv_bias,
    low_weight,
    bc_weight,
    low_gain,
    dt_weight,
    dt_bias,
    rate_log,
    skip_gain,
):
    row_count = queries.shape[0]
    count = lax.axis_size("ctx")
    head_devices = lax.axis_size("head")
    place = lax.axis_index("ctx")

    rim = lax.ppermute(mamba_in[row_count - RIM :], "ctx", [(i, i + 1) for i in range(count - 1)])

    kv_count = key_heads.shape[1] // HD
    local_kv = max(1, kv_count // head_devices)
    query_local = queries.shape[1] // HD
    group_size = query_local * head_devices // kv_count
    kv_start = lax.axis_index("head") * query_local // group_size
    near = jnp.concatenate(
        [
            lax.dynamic_slice_in_dim(key_heads, kv_start * HD, local_kv * HD, 1),
            lax.dynamic_slice_in_dim(value_heads, kv_start * HD, local_kv * HD, 1),
        ],
        axis=1,
    )
    order = [0]
    steps = bits_of(count)[::-1]
    for step in steps:
        far = swap(near, "ctx", step)
        order = order + [flip ^ step for flip in order]
        if step != steps[-1]:
            near = jnp.concatenate([near, far], axis=0)

    rates = (jnp.exp(rate_log) * -LOG2E).T
    act, part = front_call(
        mamba_in, rim, conv_weight, conv_bias[None, :], low_weight, bc_weight
    )
    steps = bits_of(head_devices)
    for step in steps:
        other = swap(part, "head", step)
        if step != steps[-1]:
            part = (part.astype(F32) + other.astype(F32)).astype(BF16)
    step_dt, ends, bc = ends_call(
        part, other, low_gain[None, :], dt_weight, dt_bias[None, :], rates, act
    )
    enter = entering(ends, rates)
    attn_out = attention_call(
        place.astype(jnp.int32)[None], span_order, block_mask, queries, near, far, tuple(order)
    )
    mamba_out = scan_call(step_dt, act, gate_in, bc, rates, enter, skip_gain[None, :])
    return (attn_out, mamba_out)


def solution(mesh):
    in_specs = (
        P("ctx", "head"),
        P("ctx", None),
        P("ctx", None),
        P(),
        P(),
        P("ctx", "head"),
        P("ctx", "head"),
        P(None, "head"),
        P("head"),
        P("head", None),
        P("head", None),
        P(),
        P(None, "head"),
        P("head"),
        P("head", None),
        P("head"),
    )
    out_specs = (P("ctx", "head"), P("ctx", "head"))
    return jax.shard_map(
        per_device, mesh=mesh, in_specs=in_specs, out_specs=out_specs, check_vma=False
    )
```

time: 295 us -> 87.8 us (0.30)
  other arithmetic: 137 us -> 6.83 us
  blocking collectives: 65.5 us -> 0 us
  Pallas kernels: 0 us -> 38.7 us
  local copies, waits for them, and re-layouts: 27.7 us -> 6.12 us
  matrix products: 15.5 us -> 0 us
  between operations: 14.1 us -> 0.77 us
  starting transfers between devices: 1.41 us -> 9.7 us
  waiting for transfers between devices: 31.6 us -> 24.1 us
    reduce_sum x73 -> x0, other arithmetic: 67.8 us -> none  [the longest x68 60.4 us: one_block(): results.append(jnp.sum(state * c_block[offset][:, None], axis=0))]
    all_gather x2 -> x0, blocking collectives: 58.4 us -> none  [the longest x1 31.7 us: attention(): lax.all_gather(value_mine, 'ctx', axis=0, tiled=True)]
    pallas_call x0 -> x4, Pallas kernels: none -> 38.7 us  [the longest x1 11.6 us: scan_call(): pl.pallas_call(scan_body, grid=(channels // width,), in_specs=[block, blo...]
    add x13 -> x0, other arithmetic: 35.3 us -> none  [the longest x4 26.5 us: one_block(): state = decay_block[offset] * state + drive_block[offset]]
    psum x1 -> x0, waiting for transfers between devices: 26.4 us -> none  [mamba(): lax.psum(low_part.astype(jnp.bfloat16), 'head').astype(jnp.float32)]
    ppermute x1 -> x9, waiting for transfers between devices: 0.01 us -> 24.1 us  [the longest x7 16.3 us: swap(): return lax.ppermute(value, axis, [(i, i ^ step) for i in range(count)])]
    dot_general x5 -> x0, matrix products: 15.5 us -> none  [the longest x1 4.67 us: attend(): jnp.einsum('rkgd,mkd->kgrm', queries4, key_split, preferred_element_type=...]
    mul x9 -> x0, local copies, waits for them, and re-layouts: 13.2 us -> none  [the longest x8 13.1 us: one_block(): results.append(jnp.sum(state * c_block[offset][:, None], axis=0))]
  transfers between devices with their start and end apart: 4 -> 9, of which waited for: 2 -> 7; matrix products, arithmetic and copies ran while one was open for 8% -> 12% of each run, Pallas kernels for 0% -> 26%
where the time goes in v1:
time: 87.8 us; the launch traced here: 86.2 us
  Pallas kernels  38.7 us (44%)
  waiting for transfers between devices  24.1 us (27%)
  starting transfers between devices  9.7 us (11%)
  other arithmetic  6.83 us (8%)
  local copies, waits for them, and re-layouts  6.12 us (7%)
    ppermute x7, waiting for transfers between devices, swap(): return lax.ppermute(value, axis, [(i, i ^ step) for i in range(count)])  16.3 us
    pallas_call x1, Pallas kernels, scan_call(): pl.pallas_call(scan_body, grid=(channels // width,), in_specs=[block, blo...  11.6 us
    pallas_call x1, Pallas kernels, ends_call(): pl.pallas_call(ends_body, grid=(channels // width,), in_specs=[whole((row...  10.8 us
    pallas_call x1, Pallas kernels, front_call(): pl.pallas_call(front_body, grid=(channels // width,), in_specs=[block, pl...  8.33 us
    pallas_call x1, Pallas kernels, attention_call(): pl.pallas_call(functools.partial(attention_body, order=order, heads=heads...  7.96 us
    ppermute x7, starting transfers between devices, swap(): return lax.ppermute(value, axis, [(i, i ^ step) for i in range(count)])  7.13 us
    ppermute x1, waiting for transfers between devices, entering(): lax.ppermute(packed, 'ctx', [(i, i ^ step) for i in range(count) if not i...  5.17 us
    unnamed x13, local copies, waits for them, and re-layouts  4.39 us
  transfers between devices with their start and end apart: 9, of which 7 were waited for; matrix products, arithmetic and copies ran while one was open for 12% of the time, Pallas kernels for 26%

profile of v1, /device:TPU:26, one launch (start us, length us, event | category | flops | bytes accessed | tf_op | source)
XLA Modules:
  0.0 86.2 jit_solution(5876203599619784157)
XLA Ops:
  1.5 1.3 %collective-permute-start.3 = (bf16[8,4096]{1,0:T(8,128)(2,1)S(1)}, bf16[8,4096]{1,0:T(8,128)(2,1)S(1)}, u32[]{:S(2)}, u32[]{:S(2)}) collective-permute-start(bf16[8,4096]{1,0:T(8,128)(2,1)S(1)} %slice.24), channel_id=1, source_target_pairs={{0,4},{4,8},{8,12},{12,16},{16,20},{20,24},{24,28},{1,5},{5,9},{9,... | collective-permute-start | bytes 196616 | tf_op jit(solution)/shard_map/ppermute | solution.py:413
  2.8 2.3 %copy.18.bc_ref = bf16[4096,32]{1,0:T(8,128)(2,1)} copy(bf16[4096,32]{0,1:T(8,128)(2,1)} %param.26) | data formatting | bytes 524288 | tf_op args[10]
  5.1 2.5 %collective-permute-done.3.rim_ref = bf16[8,4096]{1,0:T(8,128)(2,1)S(1)} collective-permute-done((bf16[8,4096]{1,0:T(8,128)(2,1)S(1)}, bf16[8,4096]{1,0:T(8,128)(2,1)S(1)}, u32[]{:S(2)}, u32[]{:S(2)}) %collective-permute-start.3) | collective-permute-done | bytes 65568 | tf_op jit(solution)/shard_map/ppermute | solution.py:413
  8.3 8.3 %front.1 = (bf16[128,4096]{1,0:T(8,128)(2,1)}, bf16[128,544]{1,0:T(8,128)(2,1)}) custom-call(bf16[128,4096]{1,0:T(8,128)(2,1)} %x_ref.1, bf16[8,4096]{1,0:T(8,128)(2,1)} %copy-done.3, f32[4,4096]{1,0:T(4,128)} %weight_ref.2, f32[1,4096]{1,0:T(1,128)} %bitcast.27, bf16[4096,512]{1,0:T(8,128)(2,1)} %low_ref.1, bf16[4096,32]{1,0:T(8,128)(2,1)} %copy.18.bc_ref), custom_call_target="tpu_custom_call" | custom-call | flops 570425344 | bytes 6553600 | tf_op jit(solution)/shard_map/front/pallas_call | solution.py:141
  16.6 0.9 %constant_dynamic-slice_fusion = (bf16[128,256]{1,0:T(8,128)(2,1)S(1)}, bf16[128,256]{1,0:T(8,128)(2,1)S(1)}) fusion(bf16[128,1024]{1,0:T(8,128)(2,1)} %param.18, s32[]{:T(128)S(6)} %select_n.56, bf16[128,1024]{1,0:T(8,128)(2,1)} %param.17), kind=kLoop, calls=%fused_computation.29 | loop fusion | bytes 262148 | tf_op jit(solution)/shard_map/dynamic_slice | solution.py:423
  18.2 1.0 %add_convert_fusion.mine_ref = bf16[128,544]{1,0:T(8,128)(2,1)S(1)} fusion(bf16[128,544]{1,0:T(8,128)(2,1)S(1)} %collective-permute-done.4, bf16[128,544]{1,0:T(8,128)(2,1)} %get-tuple-element.7), kind=kLoop, calls=%fused_computation.11 | loop fusion | flops 278528 | bytes 417792 | tf_op jit(solution)/shard_map/convert_element_type | solution.py:443
  19.2 1.6 %collective-permute-start.5 = (bf16[128,544]{1,0:T(8,128)(2,1)S(1)}, bf16[128,544]{1,0:T(8,128)(2,1)S(1)}, u32[]{:S(2)}, u32[]{:S(2)}) collective-permute-start(bf16[128,544]{1,0:T(8,128)(2,1)S(1)} %add_convert_fusion.mine_ref), channel_id=1, source_target_pairs={{0,2},{1,3},{2,0},{3,1},{4,6},{5,7},{6,4},{7,5},{8,10},{9,11},{10,... | collective-permute-start | bytes 417800 | tf_op jit(solution)/shard_map/ppermute | solution.py:24
  21.5 4.0 %collective-permute-done.5.other_ref = bf16[128,544]{1,0:T(8,128)(2,1)S(1)} collective-permute-done((bf16[128,544]{1,0:T(8,128)(2,1)S(1)}, bf16[128,544]{1,0:T(8,128)(2,1)S(1)}, u32[]{:S(2)}, u32[]{:S(2)}) %collective-permute-start.5) | collective-permute-done | bytes 139296 | tf_op jit(solution)/shard_map/ppermute | solution.py:24
  26.1 10.8 %ends.1 = (f32[128,4096]{1,0:T(8,128)}, bf16[17,4096]{1,0:T(8,128)(2,1)}, f32[128,32]{1,0:T(8,128)}) custom-call(bf16[128,544]{1,0:T(8,128)(2,1)} %copy-done.2, bf16[128,544]{1,0:T(8,128)(2,1)} %copy-done.5, f32[1,512]{1,0:T(1,128)} %bitcast.30, bf16[512,4096]{1,0:T(8,128)(2,1)} %weight_ref.3, f32[1,4096]{1,0:T(1,128)} %bitcast.28, ...), custom_call_target="tpu_custom_call" | custom-call | flops 570425344 | bytes 7340032 | tf_op jit(solution)/shard_map/ends/pallas_call | solution.py:242
  37.0 1.5 %collective-permute-start.6 = (bf16[17,4096]{1,0:T(8,128)(2,1)}, bf16[17,4096]{1,0:T(8,128)(2,1)S(1)}, u32[]{:S(2)}, u32[]{:S(2)}) collective-permute-start(bf16[17,4096]{1,0:T(8,128)(2,1)} %get-tuple-element.11), channel_id=1, source_target_pairs={{0,4},{4,0},{8,12},{12,8},{16,20},{20,16},{24,28},{28,24},{1,5},{5... | collective-permute-start | bytes 417800 | tf_op jit(solution)/shard_map/ppermute | solution.py:24
  38.5 0.9 %slice_convert_fusion.2 = f32[1,4096]{1,0:T(1,128)S(1)} fusion(bf16[17,4096]{1,0:T(8,128)(2,1)} %get-tuple-element.11), kind=kLoop, calls=%fused_computation.28 | loop fusion | flops 4096 | bytes 24576 | tf_op jit(solution)/shard_map/convert_element_type | solution.py:366
  39.3 4.0 %collective-permute-done.6 = bf16[17,4096]{1,0:T(8,128)(2,1)S(1)} collective-permute-done((bf16[17,4096]{1,0:T(8,128)(2,1)}, bf16[17,4096]{1,0:T(8,128)(2,1)S(1)}, u32[]{:S(2)}, u32[]{:S(2)}) %collective-permute-start.6) | collective-permute-done | bytes 139296 | tf_op jit(solution)/shard_map/ppermute | solution.py:24
  43.3 0.9 %fusion.7 = (bf16[1,4096]{1,0:T(2,128)(2,1)S(1)}, f32[1,4096]{1,0:T(1,128)S(1)}) fusion(bf16[17,4096]{1,0:T(8,128)(2,1)} %get-tuple-element.11, bf16[17,4096]{1,0:T(8,128)(2,1)S(1)} %collective-permute-done.6), kind=kLoop, calls=%fused_computation.32 | loop fusion | flops 16384 | bytes 40960 | tf_op jit(solution)/shard_map/convert.3
  44.2 1.1 %fusion.5 = bf16[16,4096]{1,0:T(8,128)(2,1)S(1)} fusion(f32[4096]{0:T(1024)S(1)} %bitcast.21, bf16[17,4096]{1,0:T(8,128)(2,1)} %get-tuple-element.11, f32[4096]{0:T(1024)S(1)} %bitcast.19, bf16[17,4096]{1,0:T(8,128)(2,1)S(1)} %collective-permute-done.6, pred[]{:T(512)S(6)} %ne.21, f32[4096,16]{0,1:T(8,128)S(1)} %copy-done), kind=kLoop, calls=%fused_computation.22 | loop fusion | flops 851968 | bytes 688129 | tf_op jit(solution)/shard_map/convert.2
  45.9 1.6 %collective-permute-start.1 = (bf16[256,512]{1,0:T(8,128)(2,1)S(1)}, bf16[256,512]{1,0:T(8,128)(2,1)S(1)}, u32[]{:S(2)}, u32[]{:S(2)}) collective-permute-start(bf16[256,512]{1,0:T(8,128)(2,1)S(1)} %pad_maximum_fusion.1), channel_id=1, source_target_pairs={{0,8},{4,12},{8,0},{12,4},{16,24},{20,28},{24,16},{28,20},{1,9},{5... | collective-permute-start | bytes 786440 | tf_op jit(solution)/shard_map/ppermute | solution.py:24
  47.5 5.7 %collective-permute-done.7 = bf16[17,4096]{1,0:T(8,128)(2,1)S(1)} collective-permute-done((bf16[17,4096]{1,0:T(8,128)(2,1)S(1)}, bf16[17,4096]{1,0:T(8,128)(2,1)S(1)}, u32[]{:S(2)}, u32[]{:S(2)}) %collective-permute-start.7) | collective-permute-done | bytes 139296 | tf_op jit(solution)/shard_map/ppermute | solution.py:24
  53.2 1.2 %fusion.4 = bf16[16,4096]{1,0:T(8,128)(2,1)S(1)} fusion(f32[4096]{0:T(1024)S(1)} %bitcast.26, f32[4096]{0:T(1024)S(1)} %bitcast.23, pred[]{:T(512)S(6)} %ne.20, bf16[17,4096]{1,0:T(8,128)(2,1)S(1)} %collective-permute-done.7, f32[4096]{0:T(1024)S(1)} %bitcast.22, bf16[17,4096]{1,0:T(8,128)(2,1)} %get-tuple-element.11, f32[4096]{0:T(1024)S(1)} %bitcast.20, ...), kind=kLoop, calls=%fused_computation.16 | loop fusion | flops 1507328 | bytes 851970 | tf_op jit(solution)/shard_map/convert
  54.4 1.3 %collective-permute-start.8 = (bf16[17,4096]{1,0:T(8,128)(2,1)S(1)}, bf16[17,4096]{1,0:T(8,128)(2,1)S(1)}, u32[]{:S(2)}, u32[]{:S(2)}) collective-permute-start(bf16[17,4096]{1,0:T(8,128)(2,1)S(1)} %pad_maximum_fusion.3), channel_id=1, source_target_pairs={{0,16},{4,20},{8,24},{12,28},{1,17},{5,21},{9,25},{13,29},{2,18},{... | collective-permute-start | bytes 417800 | tf_op jit(solution)/shard_map/ppermute | solution.py:376
  55.8 2.4 %collective-permute-done.1 = bf16[256,512]{1,0:T(8,128)(2,1)S(1)} collective-permute-done((bf16[256,512]{1,0:T(8,128)(2,1)S(1)}, bf16[256,512]{1,0:T(8,128)(2,1)S(1)}, u32[]{:S(2)}, u32[]{:S(2)}) %collective-permute-start.1) | collective-permute-done | bytes 262176 | tf_op jit(solution)/shard_map/ppermute | solution.py:24
  58.2 1.5 %collective-permute-start.2 = (bf16[512,512]{1,0:T(8,128)(2,1)S(1)}, bf16[512,512]{1,0:T(8,128)(2,1)S(1)}, u32[]{:S(2)}, u32[]{:S(2)}) collective-permute-start(bf16[512,512]{1,0:T(8,128)(2,1)S(1)} %pad_maximum_fusion.ka_ref.va_ref), channel_id=1, source_target_pairs={{0,4},{4,0},{8,12},{12,8},{16,20},{20,16},{24,28},{28,24},{1,5},{5... | collective-permute-start | bytes 1572872 | tf_op jit(solution)/shard_map/ppermute | solution.py:24
  59.7 5.2 %collective-permute-done.8 = bf16[17,4096]{1,0:T(8,128)(2,1)S(1)} collective-permute-done((bf16[17,4096]{1,0:T(8,128)(2,1)S(1)}, bf16[17,4096]{1,0:T(8,128)(2,1)S(1)}, u32[]{:S(2)}, u32[]{:S(2)}) %collective-permute-start.8) | collective-permute-done | bytes 139296 | tf_op jit(solution)/shard_map/ppermute | solution.py:376
  64.9 0.9 %add_select_fusion.enter_ref = f32[16,4096]{1,0:T(8,128)} fusion(bf16[17,4096]{1,0:T(8,128)(2,1)S(1)} %collective-permute-done.8, f32[4096]{0:T(1024)S(1)} %bitcast.25, f32[4096]{0:T(1024)S(1)} %bitcast.24, pred[]{:T(512)S(6)} %ne.21, pred[]{:T(512)S(6)} %ne.20, pred[]{:T(512)S(6)} %ne.19, bf16[17,4096]{1,0:T(8,128)(2,1)S(1)} %collective-permute-done.7, ...), kind=kLoop, calls=%fused_computation.1 | loop fusion | flops 1114112 | bytes 950275 | tf_op jit(solution)/shard_map/jit(_where)/select_n | solution.py:382
  65.8 11.6 %scan.1 = bf16[128,4096]{1,0:T(8,128)(2,1)} custom-call(f32[128,4096]{1,0:T(8,128)} %get-tuple-element.9.step_ref, bf16[128,4096]{1,0:T(8,128)(2,1)} %get-tuple-element.8.act_ref, bf16[128,4096]{1,0:T(8,128)(2,1)} %gate_ref.1, f32[128,32]{1,0:T(8,128)} %get-tuple-element.10.bc_ref, f32[16,4096]{1,0:T(8,128)} %multiply_bitcast_fusion.rate_ref, ...), custom_call_target="tpu_custom_call" | custom-call | flops 67108864 | bytes 5242880 | tf_op jit(solution)/shard_map/scan/pallas_call | solution.py:337
  78.2 8.0 %attention.1 = bf16[128,2048]{1,0:T(8,128)(2,1)} custom-call(s32[1]{0:T(128)} %bitcast.place, s32[16]{0:T(128)} %span_order.1, s32[16,16]{1,0:T(8,128)} %block_mask.1, bf16[128,2048]{1,0:T(8,128)(2,1)} %q_ref.1, bf16[512,512]{1,0:T(8,128)(2,1)} %copy-done.1, bf16[512,512]{1,0:T(8,128)(2,1)} %copy-done.4, bf16[512,512]{1,0:T(8,128)(2,1)} %copy-done.1, ...), custom_call_target="tpu_custom_call" | custom-call | flops 1073741824 | bytes 2097152 | tf_op jit(solution)/shard_map/attention/pallas_call | solution.py:94
  (28 shorter events, 5.1 us)
Async XLA Ops:
  1.5 6.1 %collective-permute-start.3 = (bf16[8,4096]{1,0:T(8,128)(2,1)S(1)}, bf16[8,4096]{1,0:T(8,128)(2,1)S(1)}, u32[]{:S(2)}, u32[]{:S(2)}) collective-permute-start(bf16[8,4096]{1,0:T(8,128)(2,1)S(1)} %slice.24), channel_id=1, source_target_pairs={{0,4},{4,8},{8,12},{12,16},{16,20},{20,24},{24,28},{1,5},{5,9},{9,... | collective-permute-start | bytes 196616 | tf_op jit(solution)/shard_map/ppermute | solution.py:413
  2.8 18.0 %copy-start = (f32[4096,16]{0,1:T(8,128)S(1)}, f32[4096,16]{0,1:T(8,128)}, u32[]{:S(2)}) copy-start(f32[4096,16]{0,1:T(8,128)} %param.30) | copy-start | bytes 786436
  7.6 0.6 copy-start.3
  16.6 1.6 %collective-permute-start.4 = (bf16[128,544]{1,0:T(8,128)(2,1)}, bf16[128,544]{1,0:T(8,128)(2,1)S(1)}, u32[]{:S(2)}, u32[]{:S(2)}) collective-permute-start(bf16[128,544]{1,0:T(8,128)(2,1)} %get-tuple-element.7), channel_id=1, source_target_pairs={{0,1},{1,0},{2,3},{3,2},{4,5},{5,4},{6,7},{7,6},{8,9},{9,8},{10,11... | collective-permute-start | bytes 417800 | tf_op jit(solution)/shard_map/ppermute | solution.py:24
  17.5 28.3 %collective-permute-start = (bf16[128,512]{1,0:T(8,128)(2,1)S(1)}, bf16[128,512]{1,0:T(8,128)(2,1)S(1)}, u32[]{:S(2)}, u32[]{:S(2)}) collective-permute-start(bf16[128,512]{1,0:T(8,128)(2,1)S(1)} %pad_maximum_fusion.4), channel_id=1, source_target_pairs={{0,16},{4,20},{8,24},{12,28},{16,0},{20,4},{24,8},{28,12},{1,17},{... | collective-permute-start | bytes 393224 | tf_op jit(solution)/shard_map/ppermute | solution.py:24
  19.1 6.3 %copy-start.2 = (bf16[128,544]{1,0:T(8,128)(2,1)}, bf16[128,544]{1,0:T(8,128)(2,1)S(1)}, u32[]{:S(2)}) copy-start(bf16[128,544]{1,0:T(8,128)(2,1)S(1)} %add_convert_fusion.mine_ref) | copy-start | bytes 417796
  19.2 6.3 %collective-permute-start.5 = (bf16[128,544]{1,0:T(8,128)(2,1)S(1)}, bf16[128,544]{1,0:T(8,128)(2,1)S(1)}, u32[]{:S(2)}, u32[]{:S(2)}) collective-permute-start(bf16[128,544]{1,0:T(8,128)(2,1)S(1)} %add_convert_fusion.mine_ref), channel_id=1, source_target_pairs={{0,2},{1,3},{2,0},{3,1},{4,6},{5,7},{6,4},{7,5},{8,10},{9,11},{10,... | collective-permute-start | bytes 417800 | tf_op jit(solution)/shard_map/ppermute | solution.py:24
  25.5 0.6 copy-start.5
  37.0 6.4 %collective-permute-start.6 = (bf16[17,4096]{1,0:T(8,128)(2,1)}, bf16[17,4096]{1,0:T(8,128)(2,1)S(1)}, u32[]{:S(2)}, u32[]{:S(2)}) collective-permute-start(bf16[17,4096]{1,0:T(8,128)(2,1)} %get-tuple-element.11), channel_id=1, source_target_pairs={{0,4},{4,0},{8,12},{12,8},{16,20},{20,16},{24,28},{28,24},{1,5},{5... | collective-permute-start | bytes 417800 | tf_op jit(solution)/shard_map/ppermute | solution.py:24
  45.3 7.8 %collective-permute-start.7 = (bf16[17,4096]{1,0:T(8,128)(2,1)S(1)}, bf16[17,4096]{1,0:T(8,128)(2,1)S(1)}, u32[]{:S(2)}, u32[]{:S(2)}) collective-permute-start(bf16[17,4096]{1,0:T(8,128)(2,1)S(1)} %pad_maximum_fusion.2), channel_id=1, source_target_pairs={{0,8},{4,12},{8,0},{12,4},{16,24},{20,28},{24,16},{28,20},{1,9},{5... | collective-permute-start | bytes 417800 | tf_op jit(solution)/shard_map/ppermute | solution.py:24
  45.9 12.3 %collective-permute-start.1 = (bf16[256,512]{1,0:T(8,128)(2,1)S(1)}, bf16[256,512]{1,0:T(8,128)(2,1)S(1)}, u32[]{:S(2)}, u32[]{:S(2)}) collective-permute-start(bf16[256,512]{1,0:T(8,128)(2,1)S(1)} %pad_maximum_fusion.1), channel_id=1, source_target_pairs={{0,8},{4,12},{8,0},{12,4},{16,24},{20,28},{24,16},{28,20},{1,9},{5... | collective-permute-start | bytes 786440 | tf_op jit(solution)/shard_map/ppermute | solution.py:24
  54.4 10.5 %collective-permute-start.8 = (bf16[17,4096]{1,0:T(8,128)(2,1)S(1)}, bf16[17,4096]{1,0:T(8,128)(2,1)S(1)}, u32[]{:S(2)}, u32[]{:S(2)}) collective-permute-start(bf16[17,4096]{1,0:T(8,128)(2,1)S(1)} %pad_maximum_fusion.3), channel_id=1, source_target_pairs={{0,16},{4,20},{8,24},{12,28},{1,17},{5,21},{9,25},{13,29},{2,18},{... | collective-permute-start | bytes 417800 | tf_op jit(solution)/shard_map/ppermute | solution.py:376
  58.2 19.2 %copy-start.1 = (bf16[512,512]{1,0:T(8,128)(2,1)}, bf16[512,512]{1,0:T(8,128)(2,1)S(1)}, u32[]{:S(2)}) copy-start(bf16[512,512]{1,0:T(8,128)(2,1)S(1)} %pad_maximum_fusion.ka_ref.va_ref) | copy-start | bytes 1572868
  58.2 19.2 %collective-permute-start.2 = (bf16[512,512]{1,0:T(8,128)(2,1)S(1)}, bf16[512,512]{1,0:T(8,128)(2,1)S(1)}, u32[]{:S(2)}, u32[]{:S(2)}) collective-permute-start(bf16[512,512]{1,0:T(8,128)(2,1)S(1)} %pad_maximum_fusion.ka_ref.va_ref), channel_id=1, source_target_pairs={{0,4},{4,0},{8,12},{12,8},{16,20},{20,16},{24,28},{28,24},{1,5},{5... | collective-permute-start | bytes 1572872 | tf_op jit(solution)/shard_map/ppermute | solution.py:24
  77.4 0.8 copy-start.4

commit v2 on v1

v2 whole, which is shorter than its diff:
```python
import functools

import jax
import jax.numpy as jnp
from jax import lax
from jax.experimental import pallas as pl
from jax.experimental.pallas import tpu as pltpu
from jax.sharding import PartitionSpec as P


HD = 128
STATE = 16
CONV = 4
RIM = 8
LANES = 128
TOKEN_BLOCK = 16
LOG2E = 1.4426950408889634
NEG_FILL = -1e30
F32 = jnp.float32
BF16 = jnp.bfloat16
CONTRACT_LAST = (((1,), (1,)), ((), ()))
WIDE = 40
FRONT_WIDTH = 1024
FRONT_GRANT = 55
END_BLOCK = 32


def swap(value, axis, step):
    count = lax.axis_size(axis)
    return lax.ppermute(value, axis, [(i, i ^ step) for i in range(count)])


def bits_of(count):
    steps = []
    while 2 ** len(steps) < count:
        steps.append(2 ** len(steps))
    return steps


def after(values):
    return lax.optimization_barrier(values)


def grant(mib):
    return pltpu.CompilerParams(vmem_limit_bytes=mib * 2**20)


def resident():
    return pl.BlockSpec(memory_space=pltpu.VMEM)


def cost(flops, moved, exps=0):
    return pl.CostEstimate(flops=flops, bytes_accessed=moved, transcendentals=exps)


def attention_body(
    place, span_order, block_mask, q_ref, near_ref, far_ref, *refs, order, heads, kv_head
):
    out_ref, bias = refs[-2:]
    kv_width = near_ref.shape[1] // 2
    key_lanes = pl.ds(kv_head * HD, HD)
    value_lanes = pl.ds(kv_width + kv_head * HD, HD)
    ka_ref, kb_ref = near_ref.at[:, key_lanes], far_ref.at[:, key_lanes]
    va_ref, vb_ref = near_ref.at[:, value_lanes], far_ref.at[:, value_lanes]
    half = q_ref.shape[0] // 2
    rows = 2 * half
    side = ka_ref.shape[0]

    def fill():
        me = place[0]
        row = lax.broadcasted_iota(jnp.int32, (half, rows), 0)
        col = lax.broadcasted_iota(jnp.int32, (half, rows), 1)
        lead = jnp.where(col < half, col, col - half) - row
        for query_half in range(2):
            query_span = span_order[2 * me + query_half]
            for piece, flip in enumerate(order):
                reach = []
                for key_half in range(2):
                    key_span = span_order[2 * (me ^ flip) + key_half]
                    granted = (block_mask[query_span, key_span] == 1) | (query_span == key_span)
                    reach.append(jnp.where(granted, (query_span - key_span) * half, -rows))
                limit = jnp.where(col < half, reach[0], reach[1])
                bias[query_half * half : (query_half + 1) * half, piece * rows : (piece + 1) * rows] = (
                    jnp.where(lead <= limit, 0.0, NEG_FILL)
                )

    fill()

    scale = HD ** (-0.5) * LOG2E
    for head in range(heads):
        cols = slice(head * HD, (head + 1) * HD)
        query = q_ref[:, cols]
        first = lax.dot_general(query, ka_ref[...], CONTRACT_LAST, preferred_element_type=F32)
        second = lax.dot_general(query, kb_ref[...], CONTRACT_LAST, preferred_element_type=F32)
        first = first * scale + bias[:, :side]
        second = second * scale + bias[:, side:]
        top = jnp.maximum(
            jnp.max(first, axis=1, keepdims=True), jnp.max(second, axis=1, keepdims=True)
        )
        first = jnp.exp2(first - top)
        second = jnp.exp2(second - top)
        total = jnp.sum(first, axis=1, keepdims=True) + jnp.sum(second, axis=1, keepdims=True)
        summed = jnp.dot(first.astype(BF16), va_ref[...], preferred_element_type=F32)
        summed = summed + jnp.dot(second.astype(BF16), vb_ref[...], preferred_element_type=F32)
        out_ref[:, cols] = (summed / total).astype(BF16)


def attention_call(place, span_order, block_mask, queries, near, far, so_far, turn, turns, order):
    rows, width = queries.shape
    local_kv = near.shape[1] // (2 * HD)
    heads = width // HD // turns
    kv_head = turn * local_kv // turns
    side = near.shape[0]
    smem = pl.BlockSpec(memory_space=pltpu.SMEM)
    wide = pl.BlockSpec((rows, heads * HD), lambda i: (0, turn))
    entries = rows * 2 * side * heads
    operands = [place, span_order, block_mask, queries, near, far]
    specs = [smem, smem, smem, wide, resident(), resident()]
    aliases = {}
    if so_far is not None:
        aliases = {len(operands): 0}
        operands.append(so_far)
        specs.append(pl.BlockSpec(memory_space=pl.ANY))
    return pl.pallas_call(
        functools.partial(attention_body, order=order, heads=heads, kv_head=kv_head),
        grid=(1,),
        in_specs=specs,
        out_specs=wide,
        out_shape=jax.ShapeDtypeStruct((rows, width), BF16),
        scratch_shapes=[pltpu.VMEM((rows, 2 * side), F32)],
        input_output_aliases=aliases,
        cost_estimate=cost(entries * HD * 4, 4 * rows * heads * HD + 8 * side * HD, entries),
        compiler_params=grant(WIDE),
        name="attention",
    )(*operands)


def fold_rows(table, width):
    rows, narrow = table.shape
    short = rows * narrow // width
    return jnp.concatenate([table[at : at + short] for at in range(0, rows, short)], axis=1)


def unfold_rows(folded, narrow):
    return jnp.concatenate(
        [folded[:, at : at + narrow] for at in range(0, folded.shape[1], narrow)], axis=0
    )


def front_body(*refs):
    sources, (rim_ref, act_ref, part_ref), refs = refs[:5], refs[5:8], refs[8:]
    targets, (low_sum, bc_sum, sems) = refs[:5], refs[5:]
    x_ref, weight_ref, bias_ref, low_ref, bc_ref = targets
    step = pl.program_id(0)
    width = act_ref.shape[1]
    rows = x_ref.shape[0]
    rank = low_ref.shape[1]
    here = pl.ds(pl.multiple_of(step * width, LANES), width)

    def fetches(turn):
        span = pl.ds(pl.multiple_of(turn * width, LANES), width)
        copies = []
        for index, (source, target) in enumerate(zip(sources, targets)):
            at = (span,) if target is low_ref else (slice(None), span)
            copies.append(pltpu.make_async_copy(source.at[at], target.at[at], sems.at[index, turn]))
        return copies

    @pl.when(step == 0)
    def _():
        for turn in range(sems.shape[1]):
            for copy in fetches(turn):
                copy.start()

    for copy in fetches(step):
        copy.wait()

    extended = jnp.concatenate([rim_ref[:, here].astype(F32), x_ref[:, here].astype(F32)], axis=0)
    mixed = bias_ref[:, here]
    for tap in range(CONV):
        start = RIM - (CONV - 1) + tap
        mixed = mixed + weight_ref[tap : tap + 1, here] * extended[start : start + rows, :]
    act = (mixed / (1.0 + jnp.exp(-mixed))).astype(BF16)
    act_ref[...] = act
    low = jnp.dot(act, low_ref[here, :], preferred_element_type=F32)
    bc = lax.dot_general(act, bc_ref[:, here], CONTRACT_LAST, preferred_element_type=F32)

    @pl.when(step == 0)
    def _():
        low_sum[...] = low
        bc_sum[...] = bc

    @pl.when(step > 0)
    def _():
        low_sum[...] += low
        bc_sum[...] += bc

    @pl.when(step == pl.num_programs(0) - 1)
    def _():
        part_ref[:rows, :] = low_sum[...].astype(BF16)
        part_ref[rows:, :] = fold_rows(bc_sum[...], rank).astype(BF16)


def front_call(mamba_in, rim, conv_weight, conv_bias, low_weight, bc_weight):
    rows, channels = mamba_in.shape
    rank, maps = low_weight.shape[1], bc_weight.shape[0]
    tall = rows + rows * maps // rank
    width = min(FRONT_WIDTH, channels)
    fetched = [mamba_in, conv_weight, conv_bias, low_weight, bc_weight]
    return pl.pallas_call(
        front_body,
        grid=(channels // width,),
        in_specs=[pl.BlockSpec(memory_space=pl.ANY)] * len(fetched) + [resident()],
        out_specs=[pl.BlockSpec((rows, width), lambda i: (0, i)), resident()],
        out_shape=[
            jax.ShapeDtypeStruct((rows, channels), BF16),
            jax.ShapeDtypeStruct((tall, rank), BF16),
        ],
        scratch_shapes=[
            *[pltpu.VMEM(array.shape, array.dtype) for array in fetched],
            pltpu.VMEM((rows, rank), F32),
            pltpu.VMEM((rows, maps), F32),
            pltpu.SemaphoreType.DMA((len(fetched), channels // width)),
        ],
        cost_estimate=cost(
            2 * rows * channels * (rank + maps), channels * (4 * rows + 2 * (rank + maps)), rows * channels
        ),
        compiler_params=grant(FRONT_GRANT),
        name="front",
    )(*fetched, rim)


def spread_rows(table, spread):
    rows = table.shape[0]
    tall = rows * STATE
    picker = lax.broadcasted_iota(jnp.int32, (tall, rows), 0) // STATE
    picker = picker == lax.broadcasted_iota(jnp.int32, (tall, rows), 1)
    picked = jnp.dot(picker.astype(F32).astype(BF16), table.astype(BF16), preferred_element_type=F32)
    state = lax.broadcasted_iota(jnp.int32, (tall, STATE), 0) % STATE
    kept = state == lax.broadcasted_iota(jnp.int32, (tall, STATE), 1)
    picked = jnp.where(kept, picked, 0.0).astype(BF16)
    spread[...] = jnp.dot(picked, jnp.ones((STATE, LANES), BF16), preferred_element_type=F32)


def tail_width(channels):
    return max(LANES, channels // STATE)


def sums_of(packed, channels):
    wide = tail_width(channels)
    return jnp.concatenate(
        [packed[row : row + 1, channels : channels + wide] for row in range(channels // wide)], axis=1
    )


def store_sums(ref, row, channels):
    wide = tail_width(channels)
    pieces = [row[:, at : at + wide] for at in range(0, channels, wide)]
    spare = STATE - len(pieces)
    if spare:
        pieces.append(jnp.zeros((spare, wide), F32))
    ref[:, channels:] = jnp.concatenate(pieces, axis=0).astype(BF16)


def advance(states, tiles, rates, step_ref, drive_ref, spread, base, offset, size):
    start = pl.multiple_of(base, size)
    inmap = spread[pl.ds(start * STATE + offset * STATE, STATE), :]
    moved = []
    for tile in range(tiles):
        lanes = pl.ds(tile * LANES, LANES)
        step = step_ref.at[pl.ds(start, size), lanes][pl.ds(offset, 1), :]
        drive = drive_ref.at[pl.ds(start, size), lanes][pl.ds(offset, 1), :]
        moved.append(jnp.exp2(step * rates[:, lanes]) * states[tile] + drive * inmap)
    return moved


def softplus(v):
    return jnp.maximum(v, 0.0) + jnp.log1p(jnp.exp(-jnp.abs(v)))


def rates_of(log_ref):
    return jnp.exp(log_ref[...]) * -LOG2E


def split_lanes(value):
    return [value[:, start : start + LANES] for start in range(0, value.shape[1], LANES)]


def ends_body(
    mine_ref, other_ref, gain_ref, weight_ref, bias_ref, log_ref, act_ref, step_ref, end_ref, bc_ref, normed, spread, drive, sums, rates, wide_step
):
    rows, width = act_ref.shape
    maps = bc_ref.shape[1]
    channels = sums.shape[1]
    tiles = width // LANES
    here = pl.multiple_of(pl.program_id(0) * width, LANES)

    @pl.when(pl.program_id(0) == 0)
    def _():
        both = mine_ref[...].astype(F32) + other_ref[...].astype(F32)
        low = both[:rows]
        scale = lax.rsqrt(jnp.mean(low * low, axis=1, keepdims=True) + 1e-06)
        normed[...] = (low * scale * gain_ref[...]).astype(BF16)
        bc = unfold_rows(both[rows:], maps)
        bc_ref[...] = bc
        spread_rows(bc[:, :STATE], spread)

    step = softplus(
        jnp.dot(normed[...], weight_ref[...], preferred_element_type=F32) + bias_ref[...]
    )
    wide_step[...] = step
    step_ref[...] = step.astype(BF16)
    drive[...] = step * act_ref[...].astype(F32)
    sums[:, pl.ds(here, width)] = jnp.sum(step, axis=0, keepdims=True)
    rates[...] = rates_of(log_ref)

    def block(index, states):
        states = list(states)
        for offset in range(END_BLOCK):
            states = advance(
                states, tiles, rates, wide_step, drive, spread, index * END_BLOCK, offset, END_BLOCK
            )
        return tuple(states)

    states = lax.fori_loop(
        0, rows // END_BLOCK, block, tuple(jnp.zeros((STATE, LANES), F32) for _ in range(tiles))
    )
    for tile in range(tiles):
        lanes = pl.ds(pl.multiple_of(here + tile * LANES, LANES), LANES)
        end_ref[:, lanes] = states[tile].astype(BF16)

    @pl.when(pl.program_id(0) == pl.num_programs(0) - 1)
    def _():
        store_sums(end_ref, sums[...], channels)


def ends_call(mine, other, low_gain, dt_weight, dt_bias, rate_log, act):
    rows, channels = act.shape
    tall, rank = mine.shape
    maps = (tall - rows) * rank // rows
    width = min(1024, channels)
    block = lambda height: pl.BlockSpec((height, width), lambda i: (0, i))
    whole = lambda shape: pl.BlockSpec(shape, lambda i: (0, 0))
    packed = (STATE, channels + tail_width(channels))
    return pl.pallas_call(
        ends_body,
        grid=(channels // width,),
        in_specs=[
            resident(),
            resident(),
            whole((1, rank)),
            block(rank),
            block(1),
            block(STATE),
            block(rows),
        ],
        out_specs=[block(rows), resident(), whole((rows, maps))],
        out_shape=[
            jax.ShapeDtypeStruct((rows, channels), BF16),
            jax.ShapeDtypeStruct(packed, BF16),
            jax.ShapeDtypeStruct((rows, maps), F32),
        ],
        scratch_shapes=[
            pltpu.VMEM((rows, rank), BF16),
            pltpu.VMEM((rows * STATE, LANES), F32),
            pltpu.VMEM((rows, width), F32),
            pltpu.VMEM((1, channels), F32),
            pltpu.VMEM((STATE, width), F32),
            pltpu.VMEM((rows, width), F32),
        ],
        cost_estimate=cost(
            channels * rows * (2 * rank + 4 * STATE), channels * (6 * rows + 2 * rank), rows * channels * STATE
        ),
        compiler_params=grant(WIDE),
        name="ends",
    )(mine, other, low_gain, dt_weight, dt_bias, rate_log, act)


def join_body(place, own_ref, got_ref, log_ref, out_ref, *, step):
    channels = log_ref.shape[1]
    upper = (place[0] & step) != 0
    own = own_ref[...].astype(F32)
    got = got_ref[...].astype(F32)
    early = jnp.where(upper, got, own)
    late = jnp.where(upper, own, got)
    decay = jnp.exp2(rates_of(log_ref) * sums_of(late, channels))
    out_ref[:, :channels] = (early[:, :channels] * decay + late[:, :channels]).astype(BF16)
    out_ref[:, channels:] = (early[:, channels:] + late[:, channels:]).astype(BF16)


def join_call(place, own, got, rate_log, step):
    return pl.pallas_call(
        functools.partial(join_body, step=step),
        in_specs=[pl.BlockSpec(memory_space=pltpu.SMEM), resident(), resident(), resident()],
        out_specs=resident(),
        out_shape=jax.ShapeDtypeStruct(own.shape, BF16),
        cost_estimate=cost(8 * own.size, 10 * own.size, own.size),
        compiler_params=grant(16),
        name="join",
    )(place, own, got, rate_log)


def scan_body(place, *refs, steps):
    got_refs, refs = refs[: len(steps)], refs[len(steps) :]
    step_ref, act_ref, gate_ref, bc_ref, log_ref, skip_ref, out_ref = refs[:7]
    spread, outmap, drive, enter, rates, wide_step, even, odd = refs[7:]
    rows, width = act_ref.shape
    tiles = width // LANES
    channels = enter.shape[1]
    deep = TOKEN_BLOCK * STATE
    here = pl.multiple_of(pl.program_id(0) * width, LANES)

    @pl.when(pl.program_id(0) == 0)
    def _():
        every = rates_of(log_ref)
        state = jnp.zeros((STATE, channels), F32)
        passed = jnp.zeros((1, channels), F32)
        for step, got_ref in zip(steps, got_refs):
            upper = (place[0] & step) != 0
            got = got_ref[...].astype(F32)
            state = jnp.where(upper, got[:, :channels] * jnp.exp2(every * passed) + state, state)
            passed = jnp.where(upper, sums_of(got, channels) + passed, passed)
        enter[...] = state

        spread_rows(bc_ref[:, :STATE], spread)
        place_in = lax.broadcasted_iota(jnp.int32, (STATE, deep), 1)
        repeat = (place_in % STATE) == lax.broadcasted_iota(jnp.int32, (STATE, deep), 0)
        wide = jnp.dot(
            bc_ref[:, STATE:].astype(BF16), repeat.astype(F32).astype(BF16), preferred_element_type=F32
        )
        token = lax.broadcasted_iota(jnp.int32, (rows, deep), 0) % TOKEN_BLOCK
        own = token == lax.broadcasted_iota(jnp.int32, (rows, deep), 1) // STATE
        outmap[...] = jnp.where(own, wide, 0.0).astype(BF16)

    wide_step[...] = step_ref[...].astype(F32)
    drive[...] = wide_step[...] * act_ref[...].astype(F32)
    rates[...] = jnp.exp(log_ref[:, pl.ds(here, width)]) * -LOG2E

    def walk(index, states, held):
        states = list(states)
        for offset in range(TOKEN_BLOCK):
            states = advance(
                states, tiles, rates, wide_step, drive, spread, index * TOKEN_BLOCK, offset, TOKEN_BLOCK
            )
            for tile in range(tiles):
                held[offset * STATE : (offset + 1) * STATE, tile * LANES : (tile + 1) * LANES] = states[tile]
        return tuple(states)

    def emit(index, held):
        span = pl.ds(pl.multiple_of(index * TOKEN_BLOCK, TOKEN_BLOCK), TOKEN_BLOCK)
        summed = jnp.dot(outmap[span, :], held[...].astype(BF16), preferred_element_type=F32)
        summed = summed + skip_ref[...] * act_ref[span, :].astype(F32)
        gate = gate_ref[span, :].astype(F32)
        out_ref[span, :] = (summed * (gate / (1.0 + jnp.exp(-gate)))).astype(BF16)

    def pair(index, states):
        states = walk(2 * index + 1, states, odd)
        emit(2 * index, even)
        states = walk(2 * index + 2, states, even)
        emit(2 * index + 1, odd)
        return states

    blocks = rows // TOKEN_BLOCK
    states = walk(0, split_lanes(enter[:, pl.ds(here, width)]), even)
    states = lax.fori_loop(0, blocks // 2 - 1, pair, states)
    walk(blocks - 1, states, odd)
    emit(blocks - 2, even)
    emit(blocks - 1, odd)


def scan_call(place, gots, step, act, gate, bc, rate_log, skip):
    rows, channels = act.shape
    width = min(1024, channels)
    block = lambda height: pl.BlockSpec((height, width), lambda i: (0, i))
    whole = lambda shape: pl.BlockSpec(shape, lambda i: (0, 0))
    deep = TOKEN_BLOCK * STATE
    return pl.pallas_call(
        functools.partial(scan_body, steps=bits_of(2 ** len(gots))),
        grid=(channels // width,),
        in_specs=[
            pl.BlockSpec(memory_space=pltpu.SMEM),
            *[resident() for got in gots],
            block(rows),
            block(rows),
            block(rows),
            whole(bc.shape),
            whole(rate_log.shape),
            block(1),
        ],
        out_specs=block(rows),
        out_shape=jax.ShapeDtypeStruct((rows, channels), BF16),
        scratch_shapes=[
            pltpu.VMEM((rows * STATE, LANES), F32),
            pltpu.VMEM((rows, deep), BF16),
            pltpu.VMEM((rows, width), F32),
            pltpu.VMEM((STATE, channels), F32),
            pltpu.VMEM((STATE, width), F32),
            pltpu.VMEM((rows, width), F32),
            pltpu.VMEM((deep, width), F32),
            pltpu.VMEM((deep, width), F32),
        ],
        cost_estimate=cost(8 * channels * rows * STATE, channels * rows * 10, rows * channels * STATE),
        compiler_params=grant(WIDE),
        name="scan",
    )(place, *gots, step, act, gate, bc, rate_log, skip)


def per_device(
    queries,
    key_heads,
    value_heads,
    span_order,
    block_mask,
    mamba_in,
    gate_in,
    conv_weight,
    conv_bias,
    low_weight,
    bc_weight,
    low_gain,
    dt_weight,
    dt_bias,
    rate_log,
    skip_gain,
):
    row_count = queries.shape[0]
    count = lax.axis_size("ctx")
    head_devices = lax.axis_size("head")
    place = lax.axis_index("ctx").astype(jnp.int32)[None]

    tail, key_heads, value_heads = after((mamba_in[row_count - RIM :], key_heads, value_heads))
    rim = lax.ppermute(tail, "ctx", [(i, i + 1) for i in range(count - 1)])

    kv_count = key_heads.shape[1] // HD
    local_kv = max(1, kv_count // head_devices)
    query_local = queries.shape[1] // HD
    group_size = query_local * head_devices // kv_count
    kv_start = lax.axis_index("head") * query_local // group_size
    near = jnp.concatenate(
        [
            lax.dynamic_slice_in_dim(key_heads, kv_start * HD, local_kv * HD, 1),
            lax.dynamic_slice_in_dim(value_heads, kv_start * HD, local_kv * HD, 1),
        ],
        axis=1,
    )
    kv_hops = bits_of(count)[::-1]
    kv_hops[:2] = kv_hops[:2][::-1]
    order = [0]
    for hop in kv_hops:
        order = order + [flip ^ hop for flip in order]
    far = swap(near, "ctx", kv_hops[0])

    def gather_on(near, far, turn):
        near = jnp.concatenate([near, far], axis=0)
        return near, swap(near, "ctx", kv_hops[turn])

    logs = rate_log.T
    if len(kv_hops) > 1:
        near, far = gather_on(near, far, 1)
        rim, near = after((rim, near))
    act, part = front_call(mamba_in, rim, conv_weight, conv_bias[None, :], low_weight, bc_weight.T)
    hops = bits_of(head_devices)
    for hop in hops:
        other = swap(part, "head", hop)
        if hop != hops[-1]:
            part = (part.astype(F32) + other.astype(F32)).astype(BF16)
    for turn in range(2, len(kv_hops)):
        near, far = gather_on(near, far, turn)
    step_dt, packed, bc = ends_call(
        part, other, low_gain[None, :], dt_weight, dt_bias[None, :], logs, act
    )

    attn_out = None
    gots = []
    hops = bits_of(count)
    runs = local_kv * (2 if query_local // local_kv % 2 == 0 else 1)
    for turn, hop in enumerate(hops):
        if 2 * hop == count:
            pairs = [(i, i ^ hop) for i in range(count) if not i & hop]
            got = lax.ppermute(packed, "ctx", pairs)
        else:
            got = swap(packed, "ctx", hop)
        taken = [turn] if turn + 1 < len(hops) else range(turn, runs)
        for run in taken:
            if run >= runs:
                continue
            packed, queries, near, attn_out = after((packed, queries, near, attn_out))
            attn_out = attention_call(
                place, span_order, block_mask, queries, near, far, attn_out, run, runs, tuple(order)
            )
        got, attn_out = after((got, attn_out))
        if 2 * hop < count:
            packed = join_call(place, packed, got, logs, hop)
        gots.append(got)
    mamba_out = scan_call(place, gots, step_dt, act, gate_in, bc, logs, skip_gain[None, :])
    return (attn_out, mamba_out)


def solution(mesh):
    in_specs = (
        P("ctx", "head"),
        P("ctx", None),
        P("ctx", None),
        P(),
        P(),
        P("ctx", "head"),
        P("ctx", "head"),
        P(None, "head"),
        P("head"),
        P("head", None),
        P("head", None),
        P(),
        P(None, "head"),
        P("head"),
        P("head", None),
        P("head"),
    )
    out_specs = (P("ctx", "head"), P("ctx", "head"))

    return jax.shard_map(
        per_device, mesh=mesh, in_specs=in_specs, out_specs=out_specs, check_vma=False
    )
```

time: 87.8 us -> 83.8 us (0.954)
  the two profiles are of different devices: /device:TPU:26 before, /device:TPU:0 now
where the time goes in v2:
time: 83.8 us; the launch traced here: 83.5 us
  Pallas kernels  38.6 us (46%)
  starting transfers between devices  28.6 us (34%)
  waiting for transfers between devices  10.6 us (13%)
  local copies, waits for them, and re-layouts  3.83 us (5%)
  other arithmetic  0.97 us (1%)
  between operations  0.84 us (1%)
    ppermute x7, starting transfers between devices, swap(): return lax.ppermute(value, axis, [(i, i ^ step) for i in range(count)])  18.6 us
    pallas_call x4, Pallas kernels, attention_call(): pl.pallas_call(functools.partial(attention_body, order=order, heads=heads...  11.5 us
    pallas_call x1, Pallas kernels, scan_call(): pl.pallas_call(functools.partial(scan_body, steps=bits_of(2 ** len(gots))...  11.1 us
    pallas_call x1, Pallas kernels, ends_call(): pl.pallas_call(ends_body, grid=(channels // width,), in_specs=[resident()...  8.94 us
    ppermute x7, waiting for transfers between devices, swap(): return lax.ppermute(value, axis, [(i, i ^ step) for i in range(count)])  8.73 us
    pallas_call x1, Pallas kernels, front_call(): pl.pallas_call(front_body, grid=(channels // width,), in_specs=[pl.BlockS...  6.84 us
    ppermute x1, starting transfers between devices, per_device(): got = lax.ppermute(packed, 'ctx', pairs)  6.65 us
    ppermute x1, starting transfers between devices, per_device(): rim = lax.ppermute(tail, 'ctx', [(i, i + 1) for i in range(count - 1)])  3.39 us
  transfers between devices with their start and end apart: 9, of which 5 were waited for; matrix products, arithmetic and copies ran while one was open for 1% of the time, Pallas kernels for 33%

profile of v2, /device:TPU:0, one launch (start us, length us, event | category | flops | bytes accessed | tf_op | source)
XLA Modules:
  0.0 83.5 jit_solution(14399060550524677864)
XLA Ops:
  0.7 0.9 %slice.3 = bf16[8,4096]{1,0:T(8,128)(2,1)S(1)} slice(bf16[128,4096]{1,0:T(8,128)(2,1)} %refs_0_.1), slice={[120:128], [0:4096]} | slice | bytes 131072 | tf_op jit(solution)/shard_map/slice | solution.py:530
  1.6 1.0 %constant_dynamic-slice_fusion = (bf16[128,256]{1,0:T(8,128)(2,1)S(1)}, bf16[128,256]{1,0:T(8,128)(2,1)S(1)}) fusion(bf16[128,1024]{1,0:T(8,128)(2,1)} %param.18, s32[]{:T(128)S(6)} %select_n.10, bf16[128,1024]{1,0:T(8,128)(2,1)} %param.17), kind=kLoop, calls=%fused_computation.5 | loop fusion | bytes 262148 | tf_op jit(solution)/shard_map/dynamic_slice | solution.py:541
  2.6 3.1 %collective-permute-start.1 = (bf16[128,512]{1,0:T(8,128)(2,1)S(1)}, bf16[128,512]{1,0:T(8,128)(2,1)S(1)}, u32[]{:S(2)}, u32[]{:S(2)}) collective-permute-start(bf16[128,512]{1,0:T(8,128)(2,1)S(1)} %pad_maximum_fusion.1), channel_id=1, source_target_pairs={{0,8},{4,12},{8,0},{12,4},{16,24},{20,28},{24,16},{28,20},{1,9},{5... | collective-permute-start | bytes 393224 | tf_op jit(solution)/shard_map/ppermute | solution.py:30
  5.7 3.5 %collective-permute-done.1 = bf16[128,512]{1,0:T(8,128)(2,1)S(1)} collective-permute-done((bf16[128,512]{1,0:T(8,128)(2,1)S(1)}, bf16[128,512]{1,0:T(8,128)(2,1)S(1)}, u32[]{:S(2)}, u32[]{:S(2)}) %collective-permute-start.1) | collective-permute-done | bytes 131104 | tf_op jit(solution)/shard_map/ppermute | solution.py:30
  9.3 2.8 %collective-permute-start.4 = (bf16[256,512]{1,0:T(8,128)(2,1)S(1)}, bf16[256,512]{1,0:T(8,128)(2,1)S(1)}, u32[]{:S(2)}, u32[]{:S(2)}) collective-permute-start(bf16[256,512]{1,0:T(8,128)(2,1)S(1)} %pad_maximum_fusion), channel_id=1, source_target_pairs={{0,16},{4,20},{8,24},{12,28},{16,0},{20,4},{24,8},{28,12},{1,17},{... | collective-permute-start | bytes 786440 | tf_op jit(solution)/shard_map/ppermute | solution.py:30
  12.1 3.4 %collective-permute-start = (bf16[8,4096]{1,0:T(8,128)(2,1)S(1)}, bf16[8,4096]{1,0:T(8,128)(2,1)S(1)}, u32[]{:S(2)}, u32[]{:S(2)}) collective-permute-start(bf16[8,4096]{1,0:T(8,128)(2,1)S(1)} %slice.3), channel_id=1, source_target_pairs={{0,4},{4,8},{8,12},{12,16},{16,20},{20,24},{24,28},{1,5},{5,9},{9,... | collective-permute-start | bytes 196616 | tf_op jit(solution)/shard_map/ppermute | solution.py:531
  15.5 1.9 %collective-permute-done.refs_5_ = bf16[8,4096]{1,0:T(8,128)(2,1)S(1)} collective-permute-done((bf16[8,4096]{1,0:T(8,128)(2,1)S(1)}, bf16[8,4096]{1,0:T(8,128)(2,1)S(1)}, u32[]{:S(2)}, u32[]{:S(2)}) %collective-permute-start) | collective-permute-done | bytes 65568 | tf_op jit(solution)/shard_map/ppermute | solution.py:531
  17.4 0.6 copy-done.11
  18.0 6.8 %front.1 = (bf16[128,4096]{1,0:T(8,128)(2,1)}, bf16[136,512]{1,0:T(8,128)(2,1)}) custom-call(bf16[128,4096]{1,0:T(8,128)(2,1)} %refs_0_.1, f32[4,4096]{1,0:T(4,128)} %refs_1_.1, f32[1,4096]{1,0:T(1,128)} %bitcast.15, bf16[4096,512]{1,0:T(8,128)(2,1)} %refs_3_.1, bf16[32,4096]{1,0:T(8,128)(2,1)} %bitcast.14, bf16[8,4096]{1,0:T(8,128)(2,1)} %copy-done.11), custom_call_target="tpu_custom_call" | custom-call | flops 570425344 | bytes 6553600 | tf_op jit(solution)/shard_map/front/pallas_call | solution.py:209
  25.0 2.4 %collective-permute-start.6 = (bf16[512,512]{1,0:T(8,128)(2,1)S(1)}, bf16[512,512]{1,0:T(8,128)(2,1)S(1)}, u32[]{:S(2)}, u32[]{:S(2)}) collective-permute-start(bf16[512,512]{1,0:T(8,128)(2,1)S(1)} %constant_dynamic-update-slice_fusion.near_ref), channel_id=1, source_target_pairs={{0,4},{4,0},{8,12},{12,8},{16,20},{20,16},{24,28},{28,24},{1,5},{5... | collective-permute-start | bytes 1572872 | tf_op jit(solution)/shard_map/ppermute | solution.py:30
  27.4 0.9 %add_convert_fusion.mine_ref = bf16[136,512]{1,0:T(8,128)(2,1)S(1)} fusion(bf16[136,512]{1,0:T(8,128)(2,1)S(1)} %collective-permute-done.2, bf16[136,512]{1,0:T(8,128)(2,1)} %get-tuple-element.35), kind=kLoop, calls=%fused_computation | loop fusion | flops 278528 | bytes 417792 | tf_op jit(solution)/shard_map/convert_element_type | solution.py:565
  28.3 1.6 %collective-permute-start.3 = (bf16[136,512]{1,0:T(8,128)(2,1)S(1)}, bf16[136,512]{1,0:T(8,128)(2,1)S(1)}, u32[]{:S(2)}, u32[]{:S(2)}) collective-permute-start(bf16[136,512]{1,0:T(8,128)(2,1)S(1)} %add_convert_fusion.mine_ref), channel_id=1, source_target_pairs={{0,2},{1,3},{2,0},{3,1},{4,6},{5,7},{6,4},{7,5},{8,10},{9,11},{10,... | collective-permute-start | bytes 417800 | tf_op jit(solution)/shard_map/ppermute | solution.py:30
  29.9 4.3 %collective-permute-done.3.other_ref = bf16[136,512]{1,0:T(8,128)(2,1)S(1)} collective-permute-done((bf16[136,512]{1,0:T(8,128)(2,1)S(1)}, bf16[136,512]{1,0:T(8,128)(2,1)S(1)}, u32[]{:S(2)}, u32[]{:S(2)}) %collective-permute-start.3) | collective-permute-done | bytes 139296 | tf_op jit(solution)/shard_map/ppermute | solution.py:30
  34.2 1.2 %copy-done.6 = bf16[128,4096]{1,0:T(8,128)(2,1)S(1)} copy-done((bf16[128,4096]{1,0:T(8,128)(2,1)S(1)}, bf16[128,4096]{1,0:T(8,128)(2,1)}, u32[]{:S(2)}) %copy-start.6) | copy-done | bytes 1048600
  35.5 8.9 %ends.1 = (bf16[128,4096]{1,0:T(8,128)(2,1)S(1)}, bf16[16,4352]{1,0:T(8,128)(2,1)S(1)}, f32[128,32]{1,0:T(8,128)S(1)}) custom-call(bf16[136,512]{1,0:T(8,128)(2,1)S(1)} %add_convert_fusion.mine_ref, bf16[136,512]{1,0:T(8,128)(2,1)S(1)} %collective-permute-done.3.other_ref, f32[1,512]{1,0:T(1,128)S(1)} %bitcast.13, bf16[512,4096]{1,0:T(8,128)(2,1)S(1)} %copy-done.4, ...), custom_call_target="tpu_custom_call" | custom-call | flops 570425344 | bytes 7340032 | tf_op jit(solution)/shard_map/ends/pallas_call | solution.py:344
  44.4 1.4 %collective-permute-start.5 = (bf16[16,4352]{1,0:T(8,128)(2,1)S(1)}, bf16[16,4352]{1,0:T(8,128)(2,1)S(1)}, u32[]{:S(2)}, u32[]{:S(2)}) collective-permute-start(bf16[16,4352]{1,0:T(8,128)(2,1)S(1)} %get-tuple-element.39.own_ref), channel_id=1, source_target_pairs={{0,4},{4,0},{8,12},{12,8},{16,20},{20,16},{24,28},{28,24},{1,5},{5... | collective-permute-start | bytes 417800 | tf_op jit(solution)/shard_map/ppermute | solution.py:30
  45.9 2.9 %attention.4.refs_0_ = bf16[128,2048]{1,0:T(8,128)(2,1)} custom-call(s32[1]{0:T(128)} %bitcast.place, s32[16]{0:T(128)S(1)} %copy-done.3, s32[16,16]{1,0:T(8,128)S(1)} %copy-done.2, bf16[128,2048]{1,0:T(8,128)(2,1)S(1)} %copy-done, bf16[512,512]{1,0:T(8,128)(2,1)S(1)} %constant_dynamic-update-slice_fusion.near_ref, ...), custom_call_target="tpu_custom_call" | custom-call | flops 268435456 | bytes 786432 | tf_op jit(solution)/shard_map/attention/pallas_call | solution.py:124
  48.7 0.8 collective-permute-done.5.got_ref.refs_0_
  49.7 7.1 %collective-permute-start.7 = (bf16[16,4352]{1,0:T(8,128)(2,1)S(1)}, bf16[16,4352]{1,0:T(8,128)(2,1)S(1)}, u32[]{:S(2)}, u32[]{:S(2)}) collective-permute-start(bf16[16,4352]{1,0:T(8,128)(2,1)S(1)} %join.2.own_ref), channel_id=1, source_target_pairs={{0,8},{4,12},{8,0},{12,4},{16,24},{20,28},{24,16},{28,20},{1,9},{5... | collective-permute-start | bytes 417800 | tf_op jit(solution)/shard_map/ppermute | solution.py:30
  56.8 2.9 %attention.5.refs_0_ = bf16[128,2048]{1,0:T(8,128)(2,1)} custom-call(s32[1]{0:T(128)} %bitcast.place, s32[16]{0:T(128)S(1)} %copy-done.3, s32[16,16]{1,0:T(8,128)S(1)} %copy-done.2, bf16[128,2048]{1,0:T(8,128)(2,1)S(1)} %copy-done, bf16[512,512]{1,0:T(8,128)(2,1)S(1)} %constant_dynamic-update-slice_fusion.near_ref, ...), custom_call_target="tpu_custom_call", output_to_operand_aliasing={{}: (6, {})} | custom-call | flops 268435456 | bytes 786432 | tf_op jit(solution)/shard_map/attention/pallas_call | solution.py:124
  60.0 6.6 %collective-permute-start.8 = (bf16[16,4352]{1,0:T(8,128)(2,1)S(1)}, bf16[16,4352]{1,0:T(8,128)(2,1)S(1)}, u32[]{:S(2)}, u32[]{:S(2)}) collective-permute-start(bf16[16,4352]{1,0:T(8,128)(2,1)S(1)} %join.3), channel_id=1, source_target_pairs={{0,16},{4,20},{8,24},{12,28},{1,17},{5,21},{9,25},{13,29},{2,18},{... | collective-permute-start | bytes 417800 | tf_op jit(solution)/shard_map/ppermute | solution.py:579
  66.6 2.9 %attention.6.refs_0_ = bf16[128,2048]{1,0:T(8,128)(2,1)} custom-call(s32[1]{0:T(128)} %bitcast.place, s32[16]{0:T(128)S(1)} %copy-done.3, s32[16,16]{1,0:T(8,128)S(1)} %copy-done.2, bf16[128,2048]{1,0:T(8,128)(2,1)S(1)} %copy-done, bf16[512,512]{1,0:T(8,128)(2,1)S(1)} %constant_dynamic-update-slice_fusion.near_ref, ...), custom_call_target="tpu_custom_call", output_to_operand_aliasing={{}: (6, {})} | custom-call | flops 268435456 | bytes 786432 | tf_op jit(solution)/shard_map/attention/pallas_call | solution.py:124
  69.5 2.9 %attention.7 = bf16[128,2048]{1,0:T(8,128)(2,1)} custom-call(s32[1]{0:T(128)} %bitcast.place, s32[16]{0:T(128)S(1)} %copy-done.3, s32[16,16]{1,0:T(8,128)S(1)} %copy-done.2, bf16[128,2048]{1,0:T(8,128)(2,1)S(1)} %copy-done, bf16[512,512]{1,0:T(8,128)(2,1)S(1)} %constant_dynamic-update-slice_fusion.near_ref, ...), custom_call_target="tpu_custom_call", output_to_operand_aliasing={{}: (6, {})} | custom-call | flops 268435456 | bytes 786432 | tf_op jit(solution)/shard_map/attention/pallas_call | solution.py:124
  72.4 11.1 %scan.1 = bf16[128,4096]{1,0:T(8,128)(2,1)} custom-call(s32[1]{0:T(128)} %bitcast.place, bf16[16,4352]{1,0:T(8,128)(2,1)S(1)} %collective-permute-done.5.got_ref.refs_0_, bf16[16,4352]{1,0:T(8,128)(2,1)S(1)} %collective-permute-done.7.got_ref.refs_1_, bf16[16,4352]{1,0:T(8,128)(2,1)S(1)} %collective-permute-done.8.refs_2_, ...), custom_call_target="tpu_custom_call" | custom-call | flops 67108864 | bytes 5242880 | tf_op jit(solution)/shard_map/scan/pallas_call | solution.py:476
  (34 shorter events, 0.6 us)
Async XLA Ops:
  0.6 33.6 %copy-start.1 = (f32[4096,16]{0,1:T(8,128)S(1)}, f32[4096,16]{0,1:T(8,128)}, u32[]{:S(2)}) copy-start(f32[4096,16]{0,1:T(8,128)} %param.30) | copy-start | bytes 786436
  0.6 33.6 %copy-start.8 = (f32[4096]{0:T(1024)S(1)}, f32[4096]{0:T(1024)}, u32[]{:S(2)}) copy-start(f32[4096]{0:T(1024)} %param.29) | copy-start | bytes 49156
  0.7 33.6 %copy-start.10 = (f32[512]{0:T(512)S(1)}, f32[512]{0:T(512)}, u32[]{:S(2)}) copy-start(f32[512]{0:T(512)} %param.27) | copy-start | bytes 6148
  1.6 32.7 %copy-start.4 = (bf16[512,4096]{1,0:T(8,128)(2,1)S(1)}, bf16[512,4096]{1,0:T(8,128)(2,1)}, u32[]{:S(2)}) copy-start(bf16[512,4096]{1,0:T(8,128)(2,1)} %weight_ref.1) | copy-start | bytes 12582916
  2.6 6.6 %collective-permute-start.1 = (bf16[128,512]{1,0:T(8,128)(2,1)S(1)}, bf16[128,512]{1,0:T(8,128)(2,1)S(1)}, u32[]{:S(2)}, u32[]{:S(2)}) collective-permute-start(bf16[128,512]{1,0:T(8,128)(2,1)S(1)} %pad_maximum_fusion.1), channel_id=1, source_target_pairs={{0,8},{4,12},{8,0},{12,4},{16,24},{20,28},{24,16},{28,20},{1,9},{5... | collective-permute-start | bytes 393224 | tf_op jit(solution)/shard_map/ppermute | solution.py:30
  9.3 15.7 %collective-permute-start.4 = (bf16[256,512]{1,0:T(8,128)(2,1)S(1)}, bf16[256,512]{1,0:T(8,128)(2,1)S(1)}, u32[]{:S(2)}, u32[]{:S(2)}) collective-permute-start(bf16[256,512]{1,0:T(8,128)(2,1)S(1)} %pad_maximum_fusion), channel_id=1, source_target_pairs={{0,16},{4,20},{8,24},{12,28},{16,0},{20,4},{24,8},{28,12},{1,17},{... | collective-permute-start | bytes 786440 | tf_op jit(solution)/shard_map/ppermute | solution.py:30
  12.1 5.3 %collective-permute-start = (bf16[8,4096]{1,0:T(8,128)(2,1)S(1)}, bf16[8,4096]{1,0:T(8,128)(2,1)S(1)}, u32[]{:S(2)}, u32[]{:S(2)}) collective-permute-start(bf16[8,4096]{1,0:T(8,128)(2,1)S(1)} %slice.3), channel_id=1, source_target_pairs={{0,4},{4,8},{8,12},{12,16},{16,20},{20,24},{24,28},{1,5},{5,9},{9,... | collective-permute-start | bytes 196616 | tf_op jit(solution)/shard_map/ppermute | solution.py:531
  17.4 0.6 copy-start.11
  24.8 2.6 %collective-permute-start.2 = (bf16[136,512]{1,0:T(8,128)(2,1)}, bf16[136,512]{1,0:T(8,128)(2,1)S(1)}, u32[]{:S(2)}, u32[]{:S(2)}) collective-permute-start(bf16[136,512]{1,0:T(8,128)(2,1)} %get-tuple-element.35), channel_id=1, source_target_pairs={{0,1},{1,0},{2,3},{3,2},{4,5},{5,4},{6,7},{7,6},{8,9},{9,8},{10,11... | collective-permute-start | bytes 417800 | tf_op jit(solution)/shard_map/ppermute | solution.py:30
  25.0 20.9 %collective-permute-start.6 = (bf16[512,512]{1,0:T(8,128)(2,1)S(1)}, bf16[512,512]{1,0:T(8,128)(2,1)S(1)}, u32[]{:S(2)}, u32[]{:S(2)}) collective-permute-start(bf16[512,512]{1,0:T(8,128)(2,1)S(1)} %constant_dynamic-update-slice_fusion.near_ref), channel_id=1, source_target_pairs={{0,4},{4,0},{8,12},{12,8},{16,20},{20,16},{24,28},{28,24},{1,5},{5... | collective-permute-start | bytes 1572872 | tf_op jit(solution)/shard_map/ppermute | solution.py:30
  28.3 5.9 %collective-permute-start.3 = (bf16[136,512]{1,0:T(8,128)(2,1)S(1)}, bf16[136,512]{1,0:T(8,128)(2,1)S(1)}, u32[]{:S(2)}, u32[]{:S(2)}) collective-permute-start(bf16[136,512]{1,0:T(8,128)(2,1)S(1)} %add_convert_fusion.mine_ref), channel_id=1, source_target_pairs={{0,2},{1,3},{2,0},{3,1},{4,6},{5,7},{6,4},{7,5},{8,10},{9,11},{10,... | collective-permute-start | bytes 417800 | tf_op jit(solution)/shard_map/ppermute | solution.py:30
  34.2 1.2 %copy-start.6 = (bf16[128,4096]{1,0:T(8,128)(2,1)S(1)}, bf16[128,4096]{1,0:T(8,128)(2,1)}, u32[]{:S(2)}) copy-start(bf16[128,4096]{1,0:T(8,128)(2,1)} %get-tuple-element.36.act_ref.refs_4_) | copy-start | bytes 3145732
  35.5 10.4 %copy-start = (bf16[128,2048]{1,0:T(8,128)(2,1)S(1)}, bf16[128,2048]{1,0:T(8,128)(2,1)}, u32[]{:S(2)}) copy-start(bf16[128,2048]{1,0:T(8,128)(2,1)} %q_ref.3) | copy-start | bytes 1572868
  35.5 10.4 %copy-start.2 = (s32[16,16]{1,0:T(8,128)S(1)}, s32[16,16]{1,0:T(8,128)}, u32[]{:S(2)}) copy-start(s32[16,16]{1,0:T(8,128)} %block_mask.7) | copy-start | bytes 3076
  35.5 10.4 %copy-start.3 = (s32[16]{0:T(128)S(1)}, s32[16]{0:T(128)}, u32[]{:S(2)}) copy-start(s32[16]{0:T(128)} %span_order.7) | copy-start | bytes 196
  44.4 5.1 %collective-permute-start.5 = (bf16[16,4352]{1,0:T(8,128)(2,1)S(1)}, bf16[16,4352]{1,0:T(8,128)(2,1)S(1)}, u32[]{:S(2)}, u32[]{:S(2)}) collective-permute-start(bf16[16,4352]{1,0:T(8,128)(2,1)S(1)} %get-tuple-element.39.own_ref), channel_id=1, source_target_pairs={{0,4},{4,0},{8,12},{12,8},{16,20},{20,16},{24,28},{28,24},{1,5},{5... | collective-permute-start | bytes 417800 | tf_op jit(solution)/shard_map/ppermute | solution.py:30
  49.7 22.7 %copy-start.5 = (bf16[128,4096]{1,0:T(8,128)(2,1)S(1)}, bf16[128,4096]{1,0:T(8,128)(2,1)}, u32[]{:S(2)}) copy-start(bf16[128,4096]{1,0:T(8,128)(2,1)} %refs_5_.1) | copy-start | bytes 3145732
  49.7 22.7 %copy-start.7 = (bf16[128,4096]{1,0:T(8,128)(2,1)S(1)}, bf16[128,4096]{1,0:T(8,128)(2,1)}, u32[]{:S(2)}) copy-start(bf16[128,4096]{1,0:T(8,128)(2,1)} %get-tuple-element.36.act_ref.refs_4_) | copy-start | bytes 3145732
  49.7 22.7 %copy-start.9 = (f32[4096]{0:T(1024)S(1)}, f32[4096]{0:T(1024)}, u32[]{:S(2)}) copy-start(f32[4096]{0:T(1024)} %param.31) | copy-start | bytes 49156
  49.7 10.1 %collective-permute-start.7 = (bf16[16,4352]{1,0:T(8,128)(2,1)S(1)}, bf16[16,4352]{1,0:T(8,128)(2,1)S(1)}, u32[]{:S(2)}, u32[]{:S(2)}) collective-permute-start(bf16[16,4352]{1,0:T(8,128)(2,1)S(1)} %join.2.own_ref), channel_id=1, source_target_pairs={{0,8},{4,12},{8,0},{12,4},{16,24},{20,28},{24,16},{28,20},{1,9},{5... | collective-permute-start | bytes 417800 | tf_op jit(solution)/shard_map/ppermute | solution.py:30
  60.0 12.4 %collective-permute-start.8 = (bf16[16,4352]{1,0:T(8,128)(2,1)S(1)}, bf16[16,4352]{1,0:T(8,128)(2,1)S(1)}, u32[]{:S(2)}, u32[]{:S(2)}) collective-permute-start(bf16[16,4352]{1,0:T(8,128)(2,1)S(1)} %join.3), channel_id=1, source_target_pairs={{0,16},{4,20},{8,24},{12,28},{1,17},{5,21},{9,25},{13,29},{2,18},{... | collective-permute-start | bytes 417800 | tf_op jit(solution)/shard_map/ppermute | solution.py:579

commit v3 on v2

--- a/solution.py
+++ b/solution.py
@@ -572,17 +572,17 @@
     attn_out = None
     gots = []
     hops = bits_of(count)
-    runs = local_kv * (2 if query_local // local_kv % 2 == 0 else 1)
+    halves = 2 if query_local // local_kv % 2 == 0 else 1
+    pieces = [(run, local_kv * halves) for run in range(local_kv * halves)]
+    if local_kv > 1 and halves == 2:
+        pieces = [(0, local_kv)] + pieces[2:]
     for turn, hop in enumerate(hops):
         if 2 * hop == count:
             pairs = [(i, i ^ hop) for i in range(count) if not i & hop]
             got = lax.ppermute(packed, "ctx", pairs)
         else:
             got = swap(packed, "ctx", hop)
-        taken = [turn] if turn + 1 < len(hops) else range(turn, runs)
-        for run in taken:
-            if run >= runs:
-                continue
+        for run, runs in pieces[turn : turn + 1] if 2 * hop < count else pieces[turn:]:
             packed, queries, near, attn_out = after((packed, queries, near, attn_out))
             attn_out = attention_call(
                 place, span_order, block_mask, queries, near, far, attn_out, run, runs, tuple(order)

time: 83.8 us -> 80.8 us (0.964)
  the two profiles are of different devices: /device:TPU:0 before, /device:TPU:26 now
where the time goes in v3:
time: 80.8 us; the launch traced here: 79.9 us
  Pallas kernels  37.2 us (46%)
  waiting for transfers between devices  19.8 us (25%)
  starting transfers between devices  17.2 us (21%)
  local copies, waits for them, and re-layouts  3.83 us (5%)
  other arithmetic  0.97 us (1%)
  between operations  0.83 us (1%)
    ppermute x7, starting transfers between devices, swap(): return lax.ppermute(value, axis, [(i, i ^ step) for i in range(count)])  14.7 us
    pallas_call x1, Pallas kernels, scan_call(): pl.pallas_call(functools.partial(scan_body, steps=bits_of(2 ** len(gots))...  11.1 us
    pallas_call x3, Pallas kernels, attention_call(): pl.pallas_call(functools.partial(attention_body, order=order, heads=heads...  10.1 us
    ppermute x7, waiting for transfers between devices, swap(): return lax.ppermute(value, axis, [(i, i ^ step) for i in range(count)])  9.23 us
    pallas_call x1, Pallas kernels, ends_call(): pl.pallas_call(ends_body, grid=(channels // width,), in_specs=[resident()...  8.94 us
    pallas_call x1, Pallas kernels, front_call(): pl.pallas_call(front_body, grid=(channels // width,), in_specs=[pl.BlockS...  6.85 us
    ppermute x1, waiting for transfers between devices, per_device(): got = lax.ppermute(packed, 'ctx', pairs)  5.73 us
    ppermute x1, waiting for transfers between devices, per_device(): rim = lax.ppermute(tail, 'ctx', [(i, i + 1) for i in range(count - 1)])  4.86 us
  transfers between devices with their start and end apart: 9, of which 5 were waited for; matrix products, arithmetic and copies ran while one was open for 1% of the time, Pallas kernels for 32%

profile of v3, /device:TPU:26, one launch (start us, length us, event | category | flops | bytes accessed | tf_op | source)
XLA Modules:
  0.0 79.9 jit_solution(11620983712540661797)
XLA Ops:
  0.7 0.9 %slice.3 = bf16[8,4096]{1,0:T(8,128)(2,1)S(1)} slice(bf16[128,4096]{1,0:T(8,128)(2,1)} %refs_0_.1), slice={[120:128], [0:4096]} | slice | bytes 131072 | tf_op jit(solution)/shard_map/slice | solution.py:530
  1.6 1.0 %constant_dynamic-slice_fusion = (bf16[128,256]{1,0:T(8,128)(2,1)S(1)}, bf16[128,256]{1,0:T(8,128)(2,1)S(1)}) fusion(bf16[128,1024]{1,0:T(8,128)(2,1)} %param.18, s32[]{:T(128)S(6)} %select_n.10, bf16[128,1024]{1,0:T(8,128)(2,1)} %param.17), kind=kLoop, calls=%fused_computation.5 | loop fusion | bytes 262148 | tf_op jit(solution)/shard_map/dynamic_slice | solution.py:541
  2.6 0.5 collective-permute-start.1
  3.1 4.8 %collective-permute-done.1 = bf16[128,512]{1,0:T(8,128)(2,1)S(1)} collective-permute-done((bf16[128,512]{1,0:T(8,128)(2,1)S(1)}, bf16[128,512]{1,0:T(8,128)(2,1)S(1)}, u32[]{:S(2)}, u32[]{:S(2)}) %collective-permute-start.1) | collective-permute-done | bytes 131104 | tf_op jit(solution)/shard_map/ppermute | solution.py:30
  7.9 0.4 collective-permute-start.4
  8.3 1.3 %collective-permute-start = (bf16[8,4096]{1,0:T(8,128)(2,1)S(1)}, bf16[8,4096]{1,0:T(8,128)(2,1)S(1)}, u32[]{:S(2)}, u32[]{:S(2)}) collective-permute-start(bf16[8,4096]{1,0:T(8,128)(2,1)S(1)} %slice.3), channel_id=1, source_target_pairs={{0,4},{4,8},{8,12},{12,16},{16,20},{20,24},{24,28},{1,5},{5,9},{9,... | collective-permute-start | bytes 196616 | tf_op jit(solution)/shard_map/ppermute | solution.py:531
  9.6 4.9 %collective-permute-done.refs_5_ = bf16[8,4096]{1,0:T(8,128)(2,1)S(1)} collective-permute-done((bf16[8,4096]{1,0:T(8,128)(2,1)S(1)}, bf16[8,4096]{1,0:T(8,128)(2,1)S(1)}, u32[]{:S(2)}, u32[]{:S(2)}) %collective-permute-start) | collective-permute-done | bytes 65568 | tf_op jit(solution)/shard_map/ppermute | solution.py:531
  14.5 0.6 copy-done.11
  15.1 6.8 %front.1 = (bf16[128,4096]{1,0:T(8,128)(2,1)}, bf16[136,512]{1,0:T(8,128)(2,1)}) custom-call(bf16[128,4096]{1,0:T(8,128)(2,1)} %refs_0_.1, f32[4,4096]{1,0:T(4,128)} %refs_1_.1, f32[1,4096]{1,0:T(1,128)} %bitcast.15, bf16[4096,512]{1,0:T(8,128)(2,1)} %refs_3_.1, bf16[32,4096]{1,0:T(8,128)(2,1)} %bitcast.14, bf16[8,4096]{1,0:T(8,128)(2,1)} %copy-done.11), custom_call_target="tpu_custom_call" | custom-call | flops 570425344 | bytes 6553600 | tf_op jit(solution)/shard_map/front/pallas_call | solution.py:209
  22.1 1.8 %collective-permute-start.6 = (bf16[512,512]{1,0:T(8,128)(2,1)S(1)}, bf16[512,512]{1,0:T(8,128)(2,1)S(1)}, u32[]{:S(2)}, u32[]{:S(2)}) collective-permute-start(bf16[512,512]{1,0:T(8,128)(2,1)S(1)} %constant_dynamic-update-slice_fusion.near_ref), channel_id=1, source_target_pairs={{0,4},{4,0},{8,12},{12,8},{16,20},{20,16},{24,28},{28,24},{1,5},{5... | collective-permute-start | bytes 1572872 | tf_op jit(solution)/shard_map/ppermute | solution.py:30
  23.9 0.9 %add_convert_fusion.mine_ref = bf16[136,512]{1,0:T(8,128)(2,1)S(1)} fusion(bf16[136,512]{1,0:T(8,128)(2,1)S(1)} %collective-permute-done.2, bf16[136,512]{1,0:T(8,128)(2,1)} %get-tuple-element.32), kind=kLoop, calls=%fused_computation | loop fusion | flops 278528 | bytes 417792 | tf_op jit(solution)/shard_map/convert_element_type | solution.py:565
  24.8 1.6 %collective-permute-start.3 = (bf16[136,512]{1,0:T(8,128)(2,1)S(1)}, bf16[136,512]{1,0:T(8,128)(2,1)S(1)}, u32[]{:S(2)}, u32[]{:S(2)}) collective-permute-start(bf16[136,512]{1,0:T(8,128)(2,1)S(1)} %add_convert_fusion.mine_ref), channel_id=1, source_target_pairs={{0,2},{1,3},{2,0},{3,1},{4,6},{5,7},{6,4},{7,5},{8,10},{9,11},{10,... | collective-permute-start | bytes 417800 | tf_op jit(solution)/shard_map/ppermute | solution.py:30
  26.4 4.3 %collective-permute-done.3.other_ref = bf16[136,512]{1,0:T(8,128)(2,1)S(1)} collective-permute-done((bf16[136,512]{1,0:T(8,128)(2,1)S(1)}, bf16[136,512]{1,0:T(8,128)(2,1)S(1)}, u32[]{:S(2)}, u32[]{:S(2)}) %collective-permute-start.3) | collective-permute-done | bytes 139296 | tf_op jit(solution)/shard_map/ppermute | solution.py:30
  30.7 1.2 %copy-done.6 = bf16[128,4096]{1,0:T(8,128)(2,1)S(1)} copy-done((bf16[128,4096]{1,0:T(8,128)(2,1)S(1)}, bf16[128,4096]{1,0:T(8,128)(2,1)}, u32[]{:S(2)}) %copy-start.6) | copy-done | bytes 1048600
  31.9 8.9 %ends.1 = (bf16[128,4096]{1,0:T(8,128)(2,1)S(1)}, bf16[16,4352]{1,0:T(8,128)(2,1)S(1)}, f32[128,32]{1,0:T(8,128)S(1)}) custom-call(bf16[136,512]{1,0:T(8,128)(2,1)S(1)} %add_convert_fusion.mine_ref, bf16[136,512]{1,0:T(8,128)(2,1)S(1)} %collective-permute-done.3.other_ref, f32[1,512]{1,0:T(1,128)S(1)} %bitcast.13, bf16[512,4096]{1,0:T(8,128)(2,1)S(1)} %copy-done.4, ...), custom_call_target="tpu_custom_call" | custom-call | flops 570425344 | bytes 7340032 | tf_op jit(solution)/shard_map/ends/pallas_call | solution.py:344
  40.9 1.4 %collective-permute-start.5 = (bf16[16,4352]{1,0:T(8,128)(2,1)S(1)}, bf16[16,4352]{1,0:T(8,128)(2,1)S(1)}, u32[]{:S(2)}, u32[]{:S(2)}) collective-permute-start(bf16[16,4352]{1,0:T(8,128)(2,1)S(1)} %get-tuple-element.36.own_ref), channel_id=1, source_target_pairs={{0,4},{4,0},{8,12},{12,8},{16,20},{20,16},{24,28},{28,24},{1,5},{5... | collective-permute-start | bytes 417800 | tf_op jit(solution)/shard_map/ppermute | solution.py:30
  42.4 4.3 %attention.3.refs_0_ = bf16[128,2048]{1,0:T(8,128)(2,1)} custom-call(s32[1]{0:T(128)} %bitcast.place, s32[16]{0:T(128)S(1)} %copy-done.3, s32[16,16]{1,0:T(8,128)S(1)} %copy-done.2, bf16[128,2048]{1,0:T(8,128)(2,1)S(1)} %copy-done, bf16[512,512]{1,0:T(8,128)(2,1)S(1)} %constant_dynamic-update-slice_fusion.near_ref, ...), custom_call_target="tpu_custom_call" | custom-call | flops 536870912 | bytes 1048576 | tf_op jit(solution)/shard_map/attention/pallas_call | solution.py:124
  46.8 8.9 %collective-permute-start.7 = (bf16[16,4352]{1,0:T(8,128)(2,1)S(1)}, bf16[16,4352]{1,0:T(8,128)(2,1)S(1)}, u32[]{:S(2)}, u32[]{:S(2)}) collective-permute-start(bf16[16,4352]{1,0:T(8,128)(2,1)S(1)} %join.2.own_ref), channel_id=1, source_target_pairs={{0,8},{4,12},{8,0},{12,4},{16,24},{20,28},{24,16},{28,20},{1,9},{5... | collective-permute-start | bytes 417800 | tf_op jit(solution)/shard_map/ppermute | solution.py:30
  55.7 2.9 %attention.4.refs_0_ = bf16[128,2048]{1,0:T(8,128)(2,1)} custom-call(s32[1]{0:T(128)} %bitcast.place, s32[16]{0:T(128)S(1)} %copy-done.3, s32[16,16]{1,0:T(8,128)S(1)} %copy-done.2, bf16[128,2048]{1,0:T(8,128)(2,1)S(1)} %copy-done, bf16[512,512]{1,0:T(8,128)(2,1)S(1)} %constant_dynamic-update-slice_fusion.near_ref, ...), custom_call_target="tpu_custom_call", output_to_operand_aliasing={{}: (6, {})} | custom-call | flops 268435456 | bytes 786432 | tf_op jit(solution)/shard_map/attention/pallas_call | solution.py:124
  58.6 0.2 collective-permute-done.7.got_ref.refs_1_
  58.9 1.3 %collective-permute-start.8 = (bf16[16,4352]{1,0:T(8,128)(2,1)S(1)}, bf16[16,4352]{1,0:T(8,128)(2,1)S(1)}, u32[]{:S(2)}, u32[]{:S(2)}) collective-permute-start(bf16[16,4352]{1,0:T(8,128)(2,1)S(1)} %join.3), channel_id=1, source_target_pairs={{0,16},{4,20},{8,24},{12,28},{1,17},{5,21},{9,25},{13,29},{2,18},{... | collective-permute-start | bytes 417800 | tf_op jit(solution)/shard_map/ppermute | solution.py:582
  60.2 2.9 %attention.5 = bf16[128,2048]{1,0:T(8,128)(2,1)} custom-call(s32[1]{0:T(128)} %bitcast.place, s32[16]{0:T(128)S(1)} %copy-done.3, s32[16,16]{1,0:T(8,128)S(1)} %copy-done.2, bf16[128,2048]{1,0:T(8,128)(2,1)S(1)} %copy-done, bf16[512,512]{1,0:T(8,128)(2,1)S(1)} %constant_dynamic-update-slice_fusion.near_ref, ...), custom_call_target="tpu_custom_call", output_to_operand_aliasing={{}: (6, {})} | custom-call | flops 268435456 | bytes 786432 | tf_op jit(solution)/shard_map/attention/pallas_call | solution.py:124
  63.1 5.7 %collective-permute-done.8.refs_2_ = bf16[16,4352]{1,0:T(8,128)(2,1)S(1)} collective-permute-done((bf16[16,4352]{1,0:T(8,128)(2,1)S(1)}, bf16[16,4352]{1,0:T(8,128)(2,1)S(1)}, u32[]{:S(2)}, u32[]{:S(2)}) %collective-permute-start.8) | collective-permute-done | bytes 139296 | tf_op jit(solution)/shard_map/ppermute | solution.py:582
  68.8 11.1 %scan.1 = bf16[128,4096]{1,0:T(8,128)(2,1)} custom-call(s32[1]{0:T(128)} %bitcast.place, bf16[16,4352]{1,0:T(8,128)(2,1)S(1)} %collective-permute-done.5.got_ref.refs_0_, bf16[16,4352]{1,0:T(8,128)(2,1)S(1)} %collective-permute-done.7.got_ref.refs_1_, bf16[16,4352]{1,0:T(8,128)(2,1)S(1)} %collective-permute-done.8.refs_2_, ...), custom_call_target="tpu_custom_call" | custom-call | flops 67108864 | bytes 5242880 | tf_op jit(solution)/shard_map/scan/pallas_call | solution.py:476
  (33 shorter events, 0.4 us)
Async XLA Ops:
  0.6 30.0 %copy-start.1 = (f32[4096,16]{0,1:T(8,128)S(1)}, f32[4096,16]{0,1:T(8,128)}, u32[]{:S(2)}) copy-start(f32[4096,16]{0,1:T(8,128)} %param.30) | copy-start | bytes 786436
  0.6 30.0 %copy-start.8 = (f32[4096]{0:T(1024)S(1)}, f32[4096]{0:T(1024)}, u32[]{:S(2)}) copy-start(f32[4096]{0:T(1024)} %param.29) | copy-start | bytes 49156
  0.7 30.0 %copy-start.10 = (f32[512]{0:T(512)S(1)}, f32[512]{0:T(512)}, u32[]{:S(2)}) copy-start(f32[512]{0:T(512)} %param.27) | copy-start | bytes 6148
  1.6 29.1 %copy-start.4 = (bf16[512,4096]{1,0:T(8,128)(2,1)S(1)}, bf16[512,4096]{1,0:T(8,128)(2,1)}, u32[]{:S(2)}) copy-start(bf16[512,4096]{1,0:T(8,128)(2,1)} %weight_ref.1) | copy-start | bytes 12582916
  2.6 5.3 %collective-permute-start.1 = (bf16[128,512]{1,0:T(8,128)(2,1)S(1)}, bf16[128,512]{1,0:T(8,128)(2,1)S(1)}, u32[]{:S(2)}, u32[]{:S(2)}) collective-permute-start(bf16[128,512]{1,0:T(8,128)(2,1)S(1)} %pad_maximum_fusion.1), channel_id=1, source_target_pairs={{0,8},{4,12},{8,0},{12,4},{16,24},{20,28},{24,16},{28,20},{1,9},{5... | collective-permute-start | bytes 393224 | tf_op jit(solution)/shard_map/ppermute | solution.py:30
  7.9 14.1 %collective-permute-start.4 = (bf16[256,512]{1,0:T(8,128)(2,1)S(1)}, bf16[256,512]{1,0:T(8,128)(2,1)S(1)}, u32[]{:S(2)}, u32[]{:S(2)}) collective-permute-start(bf16[256,512]{1,0:T(8,128)(2,1)S(1)} %pad_maximum_fusion), channel_id=1, source_target_pairs={{0,16},{4,20},{8,24},{12,28},{16,0},{20,4},{24,8},{28,12},{1,17},{... | collective-permute-start | bytes 786440 | tf_op jit(solution)/shard_map/ppermute | solution.py:30
  8.3 6.1 %collective-permute-start = (bf16[8,4096]{1,0:T(8,128)(2,1)S(1)}, bf16[8,4096]{1,0:T(8,128)(2,1)S(1)}, u32[]{:S(2)}, u32[]{:S(2)}) collective-permute-start(bf16[8,4096]{1,0:T(8,128)(2,1)S(1)} %slice.3), channel_id=1, source_target_pairs={{0,4},{4,8},{8,12},{12,16},{16,20},{20,24},{24,28},{1,5},{5,9},{9,... | collective-permute-start | bytes 196616 | tf_op jit(solution)/shard_map/ppermute | solution.py:531
  14.5 0.6 copy-start.11
  22.0 1.9 %collective-permute-start.2 = (bf16[136,512]{1,0:T(8,128)(2,1)}, bf16[136,512]{1,0:T(8,128)(2,1)S(1)}, u32[]{:S(2)}, u32[]{:S(2)}) collective-permute-start(bf16[136,512]{1,0:T(8,128)(2,1)} %get-tuple-element.32), channel_id=1, source_target_pairs={{0,1},{1,0},{2,3},{3,2},{4,5},{5,4},{6,7},{7,6},{8,9},{9,8},{10,11... | collective-permute-start | bytes 417800 | tf_op jit(solution)/shard_map/ppermute | solution.py:30
  22.1 20.2 %collective-permute-start.6 = (bf16[512,512]{1,0:T(8,128)(2,1)S(1)}, bf16[512,512]{1,0:T(8,128)(2,1)S(1)}, u32[]{:S(2)}, u32[]{:S(2)}) collective-permute-start(bf16[512,512]{1,0:T(8,128)(2,1)S(1)} %constant_dynamic-update-slice_fusion.near_ref), channel_id=1, source_target_pairs={{0,4},{4,0},{8,12},{12,8},{16,20},{20,16},{24,28},{28,24},{1,5},{5... | collective-permute-start | bytes 1572872 | tf_op jit(solution)/shard_map/ppermute | solution.py:30
  24.8 5.9 %collective-permute-start.3 = (bf16[136,512]{1,0:T(8,128)(2,1)S(1)}, bf16[136,512]{1,0:T(8,128)(2,1)S(1)}, u32[]{:S(2)}, u32[]{:S(2)}) collective-permute-start(bf16[136,512]{1,0:T(8,128)(2,1)S(1)} %add_convert_fusion.mine_ref), channel_id=1, source_target_pairs={{0,2},{1,3},{2,0},{3,1},{4,6},{5,7},{6,4},{7,5},{8,10},{9,11},{10,... | collective-permute-start | bytes 417800 | tf_op jit(solution)/shard_map/ppermute | solution.py:30
  30.7 1.2 %copy-start.6 = (bf16[128,4096]{1,0:T(8,128)(2,1)S(1)}, bf16[128,4096]{1,0:T(8,128)(2,1)}, u32[]{:S(2)}) copy-start(bf16[128,4096]{1,0:T(8,128)(2,1)} %get-tuple-element.33.act_ref.refs_4_) | copy-start | bytes 3145732
  31.9 10.4 %copy-start = (bf16[128,2048]{1,0:T(8,128)(2,1)S(1)}, bf16[128,2048]{1,0:T(8,128)(2,1)}, u32[]{:S(2)}) copy-start(bf16[128,2048]{1,0:T(8,128)(2,1)} %q_ref.2) | copy-start | bytes 1572868
  31.9 10.4 %copy-start.2 = (s32[16,16]{1,0:T(8,128)S(1)}, s32[16,16]{1,0:T(8,128)}, u32[]{:S(2)}) copy-start(s32[16,16]{1,0:T(8,128)} %block_mask.5) | copy-start | bytes 3076
  31.9 10.4 %copy-start.3 = (s32[16]{0:T(128)S(1)}, s32[16]{0:T(128)}, u32[]{:S(2)}) copy-start(s32[16]{0:T(128)} %span_order.5) | copy-start | bytes 196
  40.9 5.8 %collective-permute-start.5 = (bf16[16,4352]{1,0:T(8,128)(2,1)S(1)}, bf16[16,4352]{1,0:T(8,128)(2,1)S(1)}, u32[]{:S(2)}, u32[]{:S(2)}) collective-permute-start(bf16[16,4352]{1,0:T(8,128)(2,1)S(1)} %get-tuple-element.36.own_ref), channel_id=1, source_target_pairs={{0,4},{4,0},{8,12},{12,8},{16,20},{20,16},{24,28},{28,24},{1,5},{5... | collective-permute-start | bytes 417800 | tf_op jit(solution)/shard_map/ppermute | solution.py:30
  42.3 26.5 %copy-start.5 = (bf16[128,4096]{1,0:T(8,128)(2,1)S(1)}, bf16[128,4096]{1,0:T(8,128)(2,1)}, u32[]{:S(2)}) copy-start(bf16[128,4096]{1,0:T(8,128)(2,1)} %refs_5_.1) | copy-start | bytes 3145732
  42.3 26.5 %copy-start.7 = (bf16[128,4096]{1,0:T(8,128)(2,1)S(1)}, bf16[128,4096]{1,0:T(8,128)(2,1)}, u32[]{:S(2)}) copy-start(bf16[128,4096]{1,0:T(8,128)(2,1)} %get-tuple-element.33.act_ref.refs_4_) | copy-start | bytes 3145732
  42.4 26.4 %copy-start.9 = (f32[4096]{0:T(1024)S(1)}, f32[4096]{0:T(1024)}, u32[]{:S(2)}) copy-start(f32[4096]{0:T(1024)} %param.31) | copy-start | bytes 49156
  46.8 12.0 %collective-permute-start.7 = (bf16[16,4352]{1,0:T(8,128)(2,1)S(1)}, bf16[16,4352]{1,0:T(8,128)(2,1)S(1)}, u32[]{:S(2)}, u32[]{:S(2)}) collective-permute-start(bf16[16,4352]{1,0:T(8,128)(2,1)S(1)} %join.2.own_ref), channel_id=1, source_target_pairs={{0,8},{4,12},{8,0},{12,4},{16,24},{20,28},{24,16},{28,20},{1,9},{5... | collective-permute-start | bytes 417800 | tf_op jit(solution)/shard_map/ppermute | solution.py:30
  58.9 9.9 %collective-permute-start.8 = (bf16[16,4352]{1,0:T(8,128)(2,1)S(1)}, bf16[16,4352]{1,0:T(8,128)(2,1)S(1)}, u32[]{:S(2)}, u32[]{:S(2)}) collective-permute-start(bf16[16,4352]{1,0:T(8,128)(2,1)S(1)} %join.3), channel_id=1, source_target_pairs={{0,16},{4,20},{8,24},{12,28},{1,17},{5,21},{9,25},{13,29},{2,18},{... | collective-permute-start | bytes 417800 | tf_op jit(solution)/shard_map/ppermute | solution.py:582
